TPU v7x, 32 devices: a whole 2x2x4 slice. The times are simulated.
32 devices in a mesh: rep: 2 (over x), fsdp: 4 (over y, core), seq: 4 (over z).
Axes of the slice: x: 2, y: 2, z: 4, core: 2. Of those that a mesh axis runs over, the one named last changes fastest.
Arguments:
- tokens: bfloat16 [2, 16, 1024, 768], P(None, ('rep', 'fsdp'), 'seq'), may hold values from -6 to 6
- segments: int32 [2, 16, 1024], P(None, ('rep', 'fsdp')), may hold values from 0 to 1023, as said below
- positions: int32 [2, 16, 1024], P(None, ('rep', 'fsdp'), 'seq'), may hold values from 0 to 1023, as said below
- gain_attn: bfloat16 [768], P('fsdp'), may hold values from 0.5 to 1.5
- w_qkv: bfloat16 [768, 2304], P('fsdp'), may hold values from -0.21875 to 0.21875
- w_out: bfloat16 [768, 768], P('fsdp'), may hold values from -0.875 to 0.875
- gain_mlp: bfloat16 [768], P('fsdp'), may hold values from 0.5 to 1.5
- w_in: bfloat16 [768, 2304], P('fsdp'), may hold values from -0.21875 to 0.21875
- w_mlp_out: bfloat16 [1152, 768], P('fsdp'), may hold values from -0.375 to 0.375
- cotangent: bfloat16 [2, 16, 1024, 768], P(None, ('rep', 'fsdp'), 'seq'), may hold values from -6 to 6
Outputs:
- block_out: bfloat16 [2, 16, 1024, 768], P(None, ('rep', 'fsdp'), 'seq')
- input_grad: float32 [2, 16, 1024, 768], P(None, ('rep', 'fsdp'), 'seq')
- grad_gain_attn: float32 [768], P('fsdp')
- grad_qkv: float32 [768, 2304], P('fsdp')
- grad_out: float32 [768, 768], P('fsdp')
- grad_gain_mlp: float32 [768], P('fsdp')
- grad_in: float32 [768, 2304], P('fsdp')
- grad_mlp_out: float32 [1152, 768], P('fsdp')
Inputs may be any that keep to these rules, and one draw needn't show every extreme that they name: `segments`: along each sequence segment numbers start at 0, never fall and rise by one where a new document begins; documents range from a single token to the whole sequence. `positions`: each token's position is 0 at the first token of its document (as given by segments) and rises by one along the document.
All inputs are finite; a program needn't handle non-finite values.
Results may differ from a plain program's by a relative error of at most 0.02.
Values may be sent and summed in bfloat16 or wider, within the bound.
A program may use at most 192 MiB of HBM per device.

v0:
```python
import math

import jax
import jax.numpy as jnp
from jax import lax
from jax.sharding import PartitionSpec as P

D = 768
HEADS = 12
HDIM = 64
FF = 1152
HGRP = 4
MICRO = 2


eps = 1e-05
theta = 160000.0


def norm_apply(values, gain):
    mean = jnp.mean(values, axis=-1, keepdims=True)
    centered = values - mean
    var = jnp.mean(centered * centered, axis=-1, keepdims=True)
    return centered * lax.rsqrt(var + eps) * gain


def rotary_tables(pos):
    half = jnp.arange(0, HDIM, 2).astype(jnp.float32) / HDIM
    inverse = jnp.exp(-half * math.log(theta))
    angles = pos.astype(jnp.float32)[..., None] * inverse
    angles = jnp.concatenate([angles, angles], -1)
    return (jnp.cos(angles), jnp.sin(angles))


def rotate(values, cosine, sine):
    shaped = values.reshape(values.shape[:-1] + (HEADS, HDIM))
    first = shaped[..., : HDIM // 2]
    second_normalized = shaped[..., HDIM // 2 :]
    turned = jnp.concatenate([-second_normalized, first], -1)
    out = shaped * cosine[..., None, :] + turned * sine[..., None, :]
    return out.reshape(values.shape)


def unrotate(grads, cosine, sine):
    shaped = grads.reshape(grads.shape[:-1] + (HEADS, HDIM))
    turned = shaped * sine[..., None, :]
    first = turned[..., : HDIM // 2]
    second_normalized = turned[..., HDIM // 2 :]
    back = jnp.concatenate([second_normalized, -first], -1)
    out = shaped * cosine[..., None, :] + back
    return out.reshape(grads.shape)


def matmul(left, right):
    rows = left.reshape(-1, left.shape[-1])
    out = jnp.dot(rows, right, preferred_element_type=jnp.float32)
    return out.reshape(left.shape[:-1] + (right.shape[-1],))


def matmul_back(left, right):
    rows = left.reshape(-1, left.shape[-1])
    out = lax.dot_general(rows, right, (((1,), (1,)), ((), ())), preferred_element_type=jnp.float32)
    return out.reshape(left.shape[:-1] + (right.shape[0],))


def weight_grad(left, right):
    rows_left = left.reshape(-1, left.shape[-1])
    rows_right = right.reshape(-1, right.shape[-1])
    return lax.dot_general(
        rows_left, rows_right, (((0,), (0,)), ((), ())), preferred_element_type=jnp.float32
    )


def head_block(array, index):
    span = HGRP * HDIM
    piece = lax.dynamic_slice_in_dim(array, index * span, span, 2)
    return piece.reshape(array.shape[0], array.shape[1], HGRP, HDIM)


def block_scores(query_part, key_part, same):
    scores = jnp.einsum(
        "bqhd,bkhd->bhqk", query_part, key_part, preferred_element_type=jnp.float32
    ) * HDIM ** (-0.5)
    return jnp.where(same[:, None], scores, -1000000000.0)


def attend(queries, keys, values, same):
    batch, rows, width = queries.shape
    span = HGRP * HDIM

    def one(index, carry):
        attention_mixed_output, levels = carry
        scores = block_scores(head_block(queries, index), head_block(keys, index), same)
        top = jnp.max(scores, axis=-1, keepdims=True)
        total = jnp.sum(jnp.exp(scores - top), axis=-1, keepdims=True)
        level = top + jnp.log(total)
        probs = jnp.exp(scores - level).astype(jnp.bfloat16)
        part = jnp.einsum(
            "bhqk,bkhd->bqhd", probs, head_block(values, index), preferred_element_type=jnp.float32
        )
        attention_mixed_output = lax.dynamic_update_slice_in_dim(
            attention_mixed_output, part.reshape(batch, rows, span), index * span, 2
        )
        levels = lax.dynamic_update_slice_in_dim(levels, level[..., 0], index * HGRP, 1)
        return (attention_mixed_output, levels)

    start = (
        jnp.zeros((batch, rows, width), jnp.float32),
        jnp.zeros((batch, HEADS, rows), jnp.float32),
    )
    return lax.fori_loop(0, HEADS // HGRP, one, start)


def attend_back(queries, keys, values, same, levels, grad_mixed):
    batch, rows, width = queries.shape
    length = keys.shape[1]
    span = HGRP * HDIM
    scale = HDIM ** (-0.5)

    def one(index, carry):
        grad_q, grad_k, grad_v = carry
        query_part = head_block(queries, index)
        key_part = head_block(keys, index)
        grad_part = head_block(grad_mixed, index)
        scores = block_scores(query_part, key_part, same)
        level = lax.dynamic_slice_in_dim(levels, index * HGRP, HGRP, 1)[..., None]
        probs = jnp.exp(scores - level)
        low_probs = probs.astype(jnp.bfloat16)
        value_part = jnp.einsum(
            "bhqk,bqhd->bkhd", low_probs, grad_part, preferred_element_type=jnp.float32
        )
        grad_probs = jnp.einsum(
            "bqhd,bkhd->bhqk",
            grad_part,
            head_block(values, index),
            preferred_element_type=jnp.float32,
        )
        inner = jnp.sum(probs * grad_probs, axis=-1, keepdims=True)
        grad_scores = (probs * (grad_probs - inner)).astype(jnp.bfloat16)
        query_grad = (
            jnp.einsum("bhqk,bkhd->bqhd", grad_scores, key_part, preferred_element_type=jnp.float32)
            * scale
        )
        key_grad = (
            jnp.einsum(
                "bhqk,bqhd->bkhd", grad_scores, query_part, preferred_element_type=jnp.float32
            )
            * scale
        )
        grad_q = lax.dynamic_update_slice_in_dim(
            grad_q, query_grad.reshape(batch, rows, span), index * span, 2
        )
        grad_k = lax.dynamic_update_slice_in_dim(
            grad_k, key_grad.reshape(batch, length, span), index * span, 2
        )
        grad_v = lax.dynamic_update_slice_in_dim(
            grad_v, value_part.reshape(batch, length, span), index * span, 2
        )
        return (grad_q, grad_k, grad_v)

    start = (
        jnp.zeros((batch, rows, width), jnp.float32),
        jnp.zeros((batch, length, width), jnp.float32),
        jnp.zeros((batch, length, width), jnp.float32),
    )
    return lax.fori_loop(0, HEADS // HGRP, one, start)


def gelu_exact(values):
    return jax.nn.gelu(values, approximate=False)


def body(
    tokens, segments, positions, gain_attn, w_qkv, w_out, gain_mlp, w_in, w_mlp_out, cotangent
):
    shards = (gain_attn, w_qkv, w_out, gain_mlp, w_in, w_mlp_out)

    def fetch():
        return (
            lax.all_gather(shards[0], "fsdp", axis=0, tiled=True),
            lax.all_gather(shards[1], "fsdp", axis=0, tiled=True),
            lax.all_gather(shards[2], "fsdp", axis=0, tiled=True),
            lax.all_gather(shards[3], "fsdp", axis=0, tiled=True),
            lax.all_gather(shards[4], "fsdp", axis=0, tiled=True),
            lax.all_gather(shards[5], "fsdp", axis=0, tiled=True),
        )

    def add_up(totals, grads):
        if totals is None:
            return grads
        return jax.tree.map(lambda left, right: left + right, totals, grads)

    rows = tokens.shape[2]
    seq_start = lax.axis_index("seq") * rows
    totals = None
    outputs = []
    input_grads = []
    for micro in range(MICRO):
        gathered = fetch()
        gain_one = gathered[0].astype(jnp.float32)
        query_key_value_weight = gathered[1]
        output_projection_weight = gathered[2]
        gain_two = gathered[3].astype(jnp.float32)
        input_projection_weight = gathered[4]
        perceptron_weight = gathered[5]
        inputs = tokens[micro].astype(jnp.float32)
        key_segs = segments[micro]
        query_segs = lax.dynamic_slice_in_dim(key_segs, seq_start, rows, 1)
        same = query_segs[:, :, None] == key_segs[:, None, :]
        cosine, sine = rotary_tables(positions[micro])
        normed_f, norm_one_pull = jax.vjp(norm_apply, inputs, gain_one)
        normalized_input = normed_f.astype(jnp.bfloat16)
        query_key_value = matmul(normalized_input, query_key_value_weight)
        query = rotate(query_key_value[..., :D], cosine, sine).astype(jnp.bfloat16)
        key = rotate(query_key_value[..., D : 2 * D], cosine, sine).astype(jnp.bfloat16)
        value = query_key_value[..., 2 * D :].astype(jnp.bfloat16)
        all_keys, all_values = (
            lax.all_gather(key, "seq", axis=1, tiled=True),
            lax.all_gather(value, "seq", axis=1, tiled=True),
        )
        mixed_f, levels = attend(query, all_keys, all_values, same)
        attention_mixed_output = mixed_f.astype(jnp.bfloat16)
        attention_residual_sum = inputs + matmul(attention_mixed_output, output_projection_weight)
        second_f, norm_two_pull = jax.vjp(norm_apply, attention_residual_sum, gain_two)
        second_normalized = second_f.astype(jnp.bfloat16)
        hidden_activation = matmul(second_normalized, input_projection_weight)
        hidden_in = hidden_activation[..., :FF]
        hidden_gate = hidden_activation[..., FF:]
        activated, gelu_pull = jax.vjp(gelu_exact, hidden_in)
        middle_residual = (activated * hidden_gate).astype(jnp.bfloat16)
        result = attention_residual_sum + matmul(middle_residual, perceptron_weight)
        outputs.append(result.astype(jnp.bfloat16))
        gathered = fetch()
        query_key_value_weight = gathered[1]
        output_projection_weight = gathered[2]
        input_projection_weight = gathered[4]
        perceptron_weight = gathered[5]
        grad_top = cotangent[micro]
        grad_y = grad_top.astype(jnp.float32)
        grad_wmlp = weight_grad(middle_residual, grad_top)
        grad_middle = matmul_back(grad_top, perceptron_weight)
        grad_in_part = gelu_pull(grad_middle * hidden_gate)[0]
        grad_hidden = jnp.concatenate([grad_in_part, grad_middle * activated], -1).astype(
            jnp.bfloat16
        )
        grad_win = weight_grad(second_normalized, grad_hidden)
        grad_second = matmul_back(grad_hidden, input_projection_weight)
        grad_first_part, grad_gain_two = norm_two_pull(grad_second)
        grad_first = grad_y + grad_first_part
        grad_first_low = grad_first.astype(jnp.bfloat16)
        grad_wout = weight_grad(attention_mixed_output, grad_first_low)
        grad_mixed = matmul_back(grad_first_low, output_projection_weight).astype(jnp.bfloat16)
        grad_query, grad_keys, grad_values = attend_back(
            query, all_keys, all_values, same, levels, grad_mixed
        )
        grad_key, grad_value = (
            lax.psum_scatter(
                grad_keys.astype(jnp.bfloat16), "seq", scatter_dimension=1, tiled=True
            ).astype(jnp.float32),
            lax.psum_scatter(
                grad_values.astype(jnp.bfloat16), "seq", scatter_dimension=1, tiled=True
            ).astype(jnp.float32),
        )
        grad_qkv_rows = jnp.concatenate(
            [unrotate(grad_query, cosine, sine), unrotate(grad_key, cosine, sine), grad_value], -1
        ).astype(jnp.bfloat16)
        grad_wqkv = weight_grad(normalized_input, grad_qkv_rows)
        grad_normed = matmul_back(grad_qkv_rows, query_key_value_weight)
        grad_input_part, grad_gain_one = norm_one_pull(grad_normed)
        input_grads.append(grad_first + grad_input_part)
        grads = (
            jnp.sum(grad_gain_one.reshape(-1, D), axis=0),
            grad_wqkv,
            grad_wout,
            jnp.sum(grad_gain_two.reshape(-1, D), axis=0),
            grad_win,
            grad_wmlp,
        )
        totals = add_up(
            totals,
            (
                lax.psum(
                    lax.psum_scatter(
                        grads[0].astype(jnp.bfloat16), "fsdp", scatter_dimension=0, tiled=True
                    ),
                    ("rep", "seq"),
                ).astype(jnp.float32),
                lax.psum(
                    lax.psum_scatter(
                        grads[1].astype(jnp.bfloat16), "fsdp", scatter_dimension=0, tiled=True
                    ),
                    ("rep", "seq"),
                ).astype(jnp.float32),
                lax.psum(
                    lax.psum_scatter(
                        grads[2].astype(jnp.bfloat16), "fsdp", scatter_dimension=0, tiled=True
                    ),
                    ("rep", "seq"),
                ).astype(jnp.float32),
                lax.psum(
                    lax.psum_scatter(
                        grads[3].astype(jnp.bfloat16), "fsdp", scatter_dimension=0, tiled=True
                    ),
                    ("rep", "seq"),
                ).astype(jnp.float32),
                lax.psum(
                    lax.psum_scatter(
                        grads[4].astype(jnp.bfloat16), "fsdp", scatter_dimension=0, tiled=True
                    ),
                    ("rep", "seq"),
                ).astype(jnp.float32),
                lax.psum(
                    lax.psum_scatter(
                        grads[5].astype(jnp.bfloat16), "fsdp", scatter_dimension=0, tiled=True
                    ),
                    ("rep", "seq"),
                ).astype(jnp.float32),
            ),
        )
    block_out = jnp.stack(outputs, 0)
    input_grad = jnp.stack(input_grads, 0)
    return (block_out, input_grad, totals[0], totals[1], totals[2], totals[3], totals[4], totals[5])


def solution(mesh):
    placed = (
        P(None, ("rep", "fsdp"), "seq", None),
        P(None, ("rep", "fsdp"), None),
        P(None, ("rep", "fsdp"), "seq"),
        P("fsdp"),
        P("fsdp", None),
        P("fsdp", None),
        P("fsdp"),
        P("fsdp", None),
        P("fsdp", None),
        P(None, ("rep", "fsdp"), "seq", None),
    )
    return jax.shard_map(
        body,
        mesh=mesh,
        in_specs=placed,
        out_specs=(
            P(None, ("rep", "fsdp"), "seq", None),
            P(None, ("rep", "fsdp"), "seq", None),
            P("fsdp"),
            P("fsdp", None),
            P("fsdp", None),
            P("fsdp"),
            P("fsdp", None),
            P("fsdp", None),
        ),
        check_vma=False,
    )
```

profile of v0, /device:TPU:0, one launch (start us, length us, event | category | flops | bytes accessed | tf_op | source)
XLA Modules:
  0.0 1285.9 jit_solution(17867465731644877288)
XLA Ops:
  11.6 8.9 all-reduce.9
  27.6 15.4 %all-gather.9.cloned.1.call-done = bf16[768,2304]{1,0:T(8,128)(2,1)} async-done(((bf16[192,2304]{1,0:T(8,128)(2,1)}), bf16[768,2304]{1,0:T(8,128)(2,1)}) %all-gather.9.cloned.1.call-update) | async-done | bytes 3538960 | tf_op jit(solution)/shard_map/all_gather | solution.py:181
  117.2 19.9 %all-gather.13.cloned.1.call-done = bf16[2,1024,768]{2,1,0:T(8,128)(2,1)} async-done(((bf16[2,256,768]{2,1,0:T(8,128)(2,1)}), bf16[2,1024,768]{2,1,0:T(8,128)(2,1)}) %all-gather.13.cloned.1.call-update) | async-done | bytes 3145744 | tf_op jit(solution)/shard_map/all_gather | solution.py:218
  141.7 59.1 %all-gather.11.cloned.1.call-done = bf16[2,1024,768]{2,1,0:T(8,128)(2,1)} async-done(((bf16[2,256,768]{2,1,0:T(8,128)(2,1)}), bf16[2,1024,768]{2,1,0:T(8,128)(2,1)}) %all-gather.11.cloned.1.call-update) | async-done | bytes 3145744 | tf_op jit(solution)/shard_map/all_gather | solution.py:219
  205.5 50.6 %while.68 = (s32[]{:T(128)}, bf16[2,256,768]{1,2,0:T(8,128)(2,1)}, f32[2,12,256]{2,1,0:T(8,128)S(1)}, bf16[2,1024,768]{1,2,0:T(8,128)(2,1)}, bf16[2,256,768]{1,2...) while((s32[]{:T(128)}, bf16[2,256,768]{1,2,0:T(8,128)(2,1)}, ...), condition=%wide.region_5.6_spmd.clone, body=%wide.region_2.5_spmd.clone.sunk | while | flops 560461824 | bytes 68757768 | solution.py:111
  256.1 8.9 all-gather.23.cloned.1.call-done
  269.7 59.5 %all-gather.21.cloned.1.call-done = bf16[2,1024,768]{2,1,0:T(8,128)(2,1)} async-done(((bf16[2,256,768]{2,1,0:T(8,128)(2,1)}), bf16[2,1024,768]{2,1,0:T(8,128)(2,1)}) %all-gather.21.cloned.1.call-update) | async-done | bytes 3145744 | tf_op jit(solution)/shard_map/all_gather | solution.py:219
  333.8 51.2 %while.69 = (s32[]{:T(128)}, bf16[2,256,768]{1,2,0:T(8,128)(2,1)}, f32[2,12,256]{2,1,0:T(8,128)S(1)}, bf16[2,1024,768]{1,2,0:T(8,128)(2,1)}, bf16[2,256,768]{1,2...) while((s32[]{:T(128)}, bf16[2,256,768]{1,2,0:T(8,128)(2,1)}, ...), condition=%wide.region_13.14_spmd.clone, body=%wide.region_10.13_spmd.clone.sunk | while | flops 560461824 | bytes 68757768 | solution.py:111
  401.5 8.7 add_convert_fusion.1
  438.1 107.9 %while.70 = (s32[]{:T(128)}, f32[2,256,768]{1,2,0:T(8,128)}, bf16[2,1024,768]{2,1,0:T(8,128)(2,1)}, bf16[2,1024,768]{2,1,0:T(8,128)(2,1)}, bf16[2,1024,768]{1,2,...) while((s32[]{:T(128)}, f32[2,256,768]{1,2,0:T(8,128)}, ...), condition=%wide.region_20.21_spmd.clone, body=%wide.region_18.0_spmd.clone.sunk | while | flops 1375336448 | bytes 152111536 | solution.py:166
  553.3 111.0 %while.71 = (s32[]{:T(128)}, f32[2,256,768]{1,2,0:T(8,128)}, bf16[2,1024,768]{2,1,0:T(8,128)(2,1)}, bf16[2,1024,768]{2,1,0:T(8,128)(2,1)}, bf16[2,1024,768]{1,2,...) while((s32[]{:T(128)}, f32[2,256,768]{1,2,0:T(8,128)}, ...), condition=%wide.region_29.30_spmd.clone, body=%wide.region_27.0_spmd.clone.sunk | while | flops 1375336448 | bytes 152111536 | solution.py:166
  612.8 7.2 fusion.265
  713.4 18.1 %reduce-scatter.17.cloned.1.call-done = bf16[2,256,768]{2,1,0:T(8,128)(2,1)} async-done(((bf16[2,1024,768]{2,1,0:T(8,128)(2,1)}), bf16[2,256,768]{2,1,0:T(8,128)(2,1)}) %reduce-scatter.17.cloned.1.call-update) | async-done | bytes 786448 | tf_op jit(solution)/shard_map/reduce_scatter | solution.py:257
  749.3 44.7 %reduce-scatter.19.cloned.1.call-done = bf16[2,256,768]{2,1,0:T(8,128)(2,1)} async-done(((bf16[2,1024,768]{2,1,0:T(8,128)(2,1)}), bf16[2,256,768]{2,1,0:T(8,128)(2,1)}) %reduce-scatter.19.cloned.1.call-update) | async-done | bytes 786448 | tf_op jit(solution)/shard_map/reduce_scatter | solution.py:260
  799.6 22.7 %reduce-scatter.25.cloned.1.call-done = bf16[192,768]{1,0:T(8,128)(2,1)} async-done(((bf16[768,768]{1,0:T(8,128)(2,1)}), bf16[192,768]{1,0:T(8,128)(2,1)}) %reduce-scatter.25.cloned.1.call-update) | async-done | bytes 294928 | tf_op jit(solution)/shard_map/reduce_scatter | solution.py:295
  822.3 28.3 %reduce-scatter.27.cloned.1.call-done = bf16[192,768]{1,0:T(8,128)(2,1)} async-done(((bf16[768,768]{1,0:T(8,128)(2,1)}), bf16[192,768]{1,0:T(8,128)(2,1)}) %reduce-scatter.27.cloned.1.call-update) | async-done | bytes 294928 | tf_op jit(solution)/shard_map/reduce_scatter | solution.py:295
  850.6 32.4 %reduce-scatter.33.cloned.1.call-done = bf16[288,768]{1,0:T(8,128)(2,1)} async-done(((bf16[1152,768]{1,0:T(8,128)(2,1)}), bf16[288,768]{1,0:T(8,128)(2,1)}) %reduce-scatter.33.cloned.1.call-update) | async-done | bytes 442384 | tf_op jit(solution)/shard_map/reduce_scatter | solution.py:313
  883.1 32.6 %reduce-scatter.35.cloned.1.call-done = bf16[288,768]{1,0:T(8,128)(2,1)} async-done(((bf16[1152,768]{1,0:T(8,128)(2,1)}), bf16[288,768]{1,0:T(8,128)(2,1)}) %reduce-scatter.35.cloned.1.call-update) | async-done | bytes 442384 | tf_op jit(solution)/shard_map/reduce_scatter | solution.py:313
  915.7 42.8 %reduce-scatter.29.cloned.1.call-done = bf16[192,2304]{1,0:T(8,128)(2,1)} async-done(((bf16[768,2304]{1,0:T(8,128)(2,1)}), bf16[192,2304]{1,0:T(8,128)(2,1)}) %reduce-scatter.29.cloned.1.call-update) | async-done | bytes 884752 | tf_op jit(solution)/shard_map/reduce_scatter | solution.py:307
  958.5 43.0 %reduce-scatter.31.cloned.1.call-done = bf16[192,2304]{1,0:T(8,128)(2,1)} async-done(((bf16[768,2304]{1,0:T(8,128)(2,1)}), bf16[192,2304]{1,0:T(8,128)(2,1)}) %reduce-scatter.31.cloned.1.call-update) | async-done | bytes 884752 | tf_op jit(solution)/shard_map/reduce_scatter | solution.py:307
  1001.6 43.0 %reduce-scatter.21.cloned.1.call-done = bf16[192,2304]{1,0:T(8,128)(2,1)} async-done(((bf16[768,2304]{1,0:T(8,128)(2,1)}), bf16[192,2304]{1,0:T(8,128)(2,1)}) %reduce-scatter.21.cloned.1.call-update) | async-done | bytes 884752 | tf_op jit(solution)/shard_map/reduce_scatter | solution.py:289
  1044.6 43.0 %reduce-scatter.23.cloned.1.call-done = bf16[192,2304]{1,0:T(8,128)(2,1)} async-done(((bf16[768,2304]{1,0:T(8,128)(2,1)}), bf16[192,2304]{1,0:T(8,128)(2,1)}) %reduce-scatter.23.cloned.1.call-update) | async-done | bytes 884752 | tf_op jit(solution)/shard_map/reduce_scatter | solution.py:289
  1108.5 22.8 %all-reduce.6 = (bf16[192]{0:T(256)(128)(2,1)S(1)}, bf16[192]{0:T(256)(128)(2,1)S(1)}, bf16[192]{0:T(256)(128)(2,1)S(1)}, bf16[192]{0:T(256)(128)(2,1)S(1)}) all-reduce(bf16[192]{0:T(256)(128)(2,1)S(1)} %dynamic-slice.7, bf16[192]{0:T(256)(128)(2,1)S(1)} %dynamic-slice.5, ...), channel_id=1, replica_groups=mesh['rep'=2,'fsdp'=4,'seq'=4] {'rep','seq'}, use_global_device_ids=true, to_apply=%region_39.40 | all-reduce | flops 768 | bytes 3072 | tf_op jit(solution)/shard_map/psum | solution.py:282
  1138.0 134.8 %all-reduce.12.cloned.1.call-done = (bf16[192,2304]{1,0:T(8,128)(2,1)}, bf16[192,2304]{1,0:T(8,128)(2,1)}, bf16[192,768]{1,0:T(8,128)(2,1)}, bf16[192,768]{1,0:T...) async-done(((bf16[192,2304]{1,0:T(8,128)(2,1)}, bf16[192,2304]{1,0:T(8,128)(2,1)}, ...) | async-done | bytes 5013520 | tf_op jit(solution)/shard_map/psum | solution.py:288
  (634 shorter events, 571.0 us)
Async XLA Ops:
  7.2 35.9 %all-gather.9.cloned.1.call-start = ((), (), s32[]{:S(2)}) async-start(), calls=%async_computation.12 | async-start | bytes 4423680 | tf_op jit(solution)/shard_map/all_gather | solution.py:181
  7.9 129.1 %all-gather.13.cloned.1.call-start = ((), (), s32[]{:S(2)}) async-start(), calls=%async_computation.14 | async-start | bytes 3932160 | tf_op jit(solution)/shard_map/all_gather | solution.py:218
  20.6 58.7 %copy-start.74 = (f32[768]{0:T(1024)}, f32[768]{0:T(1024)S(1)}, u32[]{:S(2)}) copy-start(f32[768]{0:T(1024)S(1)} %convert_element_type.268) | copy-start | bytes 9220
  22.4 73.1 %copy-start.50 = (f32[2,256,64]{1,2,0:T(8,128)}, f32[2,256,64]{1,2,0:T(8,128)S(1)}, u32[]{:S(2)}) copy-start(f32[2,256,64]{1,2,0:T(8,128)S(1)} %get-tuple-element.1030) | copy-start | bytes 393220
  73.4 127.4 %all-gather.11.cloned.1.call-start = ((), (), s32[]{:S(2)}) async-start(), calls=%async_computation.13 | async-start | bytes 3932160 | tf_op jit(solution)/shard_map/all_gather | solution.py:219
  75.9 189.1 %all-gather.23.cloned.1.call-start = ((), (), s32[]{:S(2)}) async-start(), calls=%async_computation.19 | async-start | bytes 3932160 | tf_op jit(solution)/shard_map/all_gather | solution.py:218
  108.1 221.1 %all-gather.21.cloned.1.call-start = ((), (), s32[]{:S(2)}) async-start(), calls=%async_computation.18 | async-start | bytes 3932160 | tf_op jit(solution)/shard_map/all_gather | solution.py:219
  110.5 274.5 %all-gather.15.cloned.1.call-start = ((), (), s32[]{:S(2)}) async-start(), calls=%async_computation.15 | async-start | bytes 1474560 | tf_op jit(solution)/shard_map/all_gather | solution.py:182
  111.1 279.0 %all-gather.17.cloned.1.call-start = ((), (), s32[]{:S(2)}) async-start(), calls=%async_computation.16 | async-start | bytes 4423680 | tf_op jit(solution)/shard_map/all_gather | solution.py:184
  111.9 289.6 %all-gather.19.cloned.1.call-start = ((), (), s32[]{:S(2)}) async-start(), calls=%async_computation.17 | async-start | bytes 2211840 | tf_op jit(solution)/shard_map/all_gather | solution.py:185
  112.6 579.9 %reduce-scatter.13.cloned.1.call-start = ((), (), s32[]{:S(2)}) async-start(), calls=%async_computation.20 | async-start | bytes 3932160 | tf_op jit(solution)/shard_map/reduce_scatter | solution.py:257
  114.8 313.9 %copy-start.95 = (f32[768]{0:T(1024)}, f32[768]{0:T(1024)S(1)}, u32[]{:S(2)}) copy-start(f32[768]{0:T(1024)S(1)} %convert_element_type.276) | copy-start | bytes 9220
  546.0 158.8 %reduce-scatter.15.cloned.1.call-start = ((), (), s32[]{:S(2)}) async-start(), calls=%async_computation.21 | async-start | bytes 3932160 | tf_op jit(solution)/shard_map/reduce_scatter | solution.py:260
  546.6 184.9 %reduce-scatter.17.cloned.1.call-start = ((), (), s32[]{:S(2)}) async-start(), calls=%async_computation.22 | async-start | bytes 3932160 | tf_op jit(solution)/shard_map/reduce_scatter | solution.py:257
  664.3 129.7 %reduce-scatter.19.cloned.1.call-start = ((), (), s32[]{:S(2)}) async-start(), calls=%async_computation.23 | async-start | bytes 3932160 | tf_op jit(solution)/shard_map/reduce_scatter | solution.py:260
  664.9 157.4 %reduce-scatter.25.cloned.1.call-start = ((), (), s32[]{:S(2)}) async-start(), calls=%async_computation.26 | async-start | bytes 1474560 | tf_op jit(solution)/shard_map/reduce_scatter | solution.py:295
  667.5 183.1 %reduce-scatter.27.cloned.1.call-start = ((), (), s32[]{:S(2)}) async-start(), calls=%async_computation.27 | async-start | bytes 1474560 | tf_op jit(solution)/shard_map/reduce_scatter | solution.py:295
  669.4 213.7 %reduce-scatter.33.cloned.1.call-start = ((), (), s32[]{:S(2)}) async-start(), calls=%async_computation.30 | async-start | bytes 2211840 | tf_op jit(solution)/shard_map/reduce_scatter | solution.py:313
  673.0 242.7 %reduce-scatter.35.cloned.1.call-start = ((), (), s32[]{:S(2)}) async-start(), calls=%async_computation.31 | async-start | bytes 2211840 | tf_op jit(solution)/shard_map/reduce_scatter | solution.py:313
  676.9 281.7 %reduce-scatter.29.cloned.1.call-start = ((), (), s32[]{:S(2)}) async-start(), calls=%async_computation.28 | async-start | bytes 4423680 | tf_op jit(solution)/shard_map/reduce_scatter | solution.py:307
  682.4 319.1 %reduce-scatter.31.cloned.1.call-start = ((), (), s32[]{:S(2)}) async-start(), calls=%async_computation.29 | async-start | bytes 4423680 | tf_op jit(solution)/shard_map/reduce_scatter | solution.py:307
  689.5 355.1 %reduce-scatter.21.cloned.1.call-start = ((), (), s32[]{:S(2)}) async-start(), calls=%async_computation.24 | async-start | bytes 4423680 | tf_op jit(solution)/shard_map/reduce_scatter | solution.py:289
  710.4 377.2 %reduce-scatter.23.cloned.1.call-start = ((), (), s32[]{:S(2)}) async-start(), calls=%async_computation.25 | async-start | bytes 4423680 | tf_op jit(solution)/shard_map/reduce_scatter | solution.py:289
  799.5 473.3 %all-reduce.12.cloned.1.call-start = ((), (), s32[]{:S(2)}) async-start(), calls=%async_computation.32 | async-start | bytes 10027008 | tf_op jit(solution)/shard_map/psum | solution.py:288
  (145 other events, 1052.1 us)
Sparse Core Ops, SparseCore 0:
  9.6 33.4 all-gather.8
  73.5 63.4 all-gather.12
  138.6 62.1 all-gather.10
  202.8 62.1 all-gather.22
  267.0 62.1 all-gather.20
  330.6 16.1 all-gather.14
  348.3 30.7 all-gather.16
  380.7 20.7 all-gather.18
  546.1 60.2 reduce-scatter.12
  608.5 60.2 reduce-scatter.14
  671.2 60.2 reduce-scatter.16
  733.7 60.2 reduce-scatter.18
  796.6 25.7 reduce-scatter.24
  824.9 25.7 reduce-scatter.26
  853.6 29.3 reduce-scatter.32
  886.3 29.3 reduce-scatter.34
  918.1 40.3 reduce-scatter.28
  961.1 40.4 reduce-scatter.30
  1004.1 40.4 reduce-scatter.20
  1047.2 40.4 reduce-scatter.22
  1092.1 180.6 all-reduce.11
where the time goes:
time: 1290 us
  waiting for transfers between devices  657 us (51%)
  matrix products  257 us (20%)
  local copies, waits for them, and re-layouts  219 us (17%)
  other arithmetic  94.1 us (7%)
  blocking collectives  37.9 us (3%)
  between operations  17.3 us (1%)
    psum x1, waiting for transfers between devices, body(): lax.psum(lax.psum_scatter(grads[1].astype(jnp.bfloat16), 'fsdp', scatter_...  135 us
    all_gather x2, waiting for transfers between devices, body(): lax.all_gather(value, 'seq', axis=1, tiled=True)  119 us
    reduce_scatter x2, waiting for transfers between devices, body(): lax.psum_scatter(grads[1].astype(jnp.bfloat16), 'fsdp', scatter_dimension...  86.1 us
    reduce_scatter x2, waiting for transfers between devices, body(): lax.psum_scatter(grads[4].astype(jnp.bfloat16), 'fsdp', scatter_dimension...  85.9 us
    reduce_scatter x2, waiting for transfers between devices, body(): lax.psum_scatter(grads[5].astype(jnp.bfloat16), 'fsdp', scatter_dimension...  65 us
    reduce_scatter x2, waiting for transfers between devices, body(): lax.psum_scatter(grads[2].astype(jnp.bfloat16), 'fsdp', scatter_dimension...  51.1 us
    reduce_scatter x2, waiting for transfers between devices, body(): lax.psum_scatter(grad_values.astype(jnp.bfloat16), 'seq', scatter_dimensi...  44.7 us
    dynamic_slice x42, local copies, waits for them, and re-layouts, head_block(): piece = lax.dynamic_slice_in_dim(array, index * span, span, 2)  40.7 us
  transfers between devices with their start and end apart: 21, of which 17 were waited for; matrix products, arithmetic and copies ran while one was open for 28% of the time, Pallas kernels for 0%

commit v1 on v0

v1 whole, which is shorter than its diff:
```python
import functools
import math

import jax
import jax.numpy as jnp
from jax import lax
from jax.experimental import pallas as pl
from jax.experimental.pallas import tpu as pltpu
from jax.sharding import PartitionSpec as P

D = 768
HEADS = 12
HDIM = 64
FF = 1152
EPS = 1e-05
THETA = 160000.0
MASKED = -1000000000.0
TILE = 256
PAIR = 2 * HDIM
HCHUNK = 384
f32 = jnp.float32
bf16 = jnp.bfloat16
VMEM_LIMIT = 56 * 2**20


def dot_nn(left, right):
    return lax.dot_general(left, right, (((1,), (0,)), ((), ())), preferred_element_type=f32)


def dot_nt(left, right):
    return lax.dot_general(left, right, (((1,), (1,)), ((), ())), preferred_element_type=f32)


def dot_tn(left, right):
    return lax.dot_general(left, right, (((0,), (0,)), ((), ())), preferred_element_type=f32)


def normalize(values):
    mean = jnp.mean(values, axis=-1, keepdims=True)
    centered = values - mean
    var = jnp.mean(centered * centered, axis=-1, keepdims=True)
    scale = lax.rsqrt(var + EPS)
    return centered * scale, scale


def norm_back(unit, scale, gain, grad):
    gain_terms = grad * unit
    inner = grad * gain
    first = jnp.mean(inner, axis=-1, keepdims=True)
    second = jnp.mean(inner * unit, axis=-1, keepdims=True)
    return scale * (inner - first - unit * second), gain_terms


def lane_halves(shape):
    lane = lax.broadcasted_iota(jnp.int32, shape, len(shape) - 1)
    return lane % HDIM < HDIM // 2


def rotate_pair(values, cosine, signed_sine):
    swapped = jnp.where(
        lane_halves(values.shape),
        pltpu.roll(values, PAIR - HDIM // 2, 1),
        pltpu.roll(values, HDIM // 2, 1),
    )
    return values * cosine + swapped * signed_sine


def first_kernel(x_ref, gain_ref, w_ref, cos_ref, sin_ref, a_ref, qkv_ref):
    unit, _ = normalize(x_ref[...].astype(f32))
    a = (unit * gain_ref[...]).astype(bf16)
    a_ref[...] = a
    cosine, sine = cos_ref[...], sin_ref[...]
    for column in range(0, 3 * D, TILE):
        part = dot_nn(a, w_ref[:, column : column + TILE])
        for half in range(0, TILE, PAIR):
            start = column + half
            piece = part[:, half : half + PAIR]
            if start < 2 * D:
                piece = rotate_pair(piece, cosine, sine)
            if start < D:
                piece = piece * HDIM**-0.5
            qkv_ref[:, start : start + PAIR] = piece.astype(bf16)


def attend_kernel(q_ref, k_ref, v_ref, rows_ref, cols_ref, o_ref, p_ref):
    k, v = k_ref[...], v_ref[...]
    lane = lax.broadcasted_iota(jnp.int32, (1, PAIR), 1)
    length = k.shape[0]
    for tile in range(0, length, TILE):
        q = q_ref[tile : tile + TILE, :]
        same = rows_ref[tile : tile + TILE, :] == cols_ref[...]
        out = None
        for head in range(2):
            mine = (lane < HDIM) if head == 0 else (lane >= HDIM)
            zero = jnp.zeros((), bf16)
            scores = dot_nt(jnp.where(mine, q, zero), k)
            scores = jnp.where(same, scores, MASKED)
            top = jnp.max(scores, axis=-1, keepdims=True)
            raised = jnp.exp(scores - top)
            total = jnp.sum(raised, axis=-1, keepdims=True)
            probs = (raised * (1.0 / total)).astype(bf16)
            p_ref[head, tile : tile + TILE, :] = probs
            part = dot_nn(probs, jnp.where(mine, v, zero))
            out = part if out is None else out + part
        o_ref[tile : tile + TILE, :] = out.astype(bf16)


def middle_kernel(
    o_ref, x_ref, gain_ref, w_out_ref, w_in_ref, w_mlp_ref,
    x1_ref, b_ref, m_ref, slope_ref, act_ref, y_ref,
):
    x1 = x_ref[...].astype(f32) + dot_nn(o_ref[...], w_out_ref[...])
    x1_ref[...] = x1
    unit, _ = normalize(x1)
    b = (unit * gain_ref[...]).astype(bf16)
    b_ref[...] = b
    y = x1
    for column in range(0, FF, HCHUNK):
        hin = dot_nn(b, w_in_ref[:, column : column + HCHUNK])
        gate = dot_nn(b, w_in_ref[:, FF + column : FF + column + HCHUNK])
        phi = 0.5 + 0.5 * lax.erf(hin * math.sqrt(0.5))
        act = hin * phi
        slope = phi + hin * (jnp.exp(hin * hin * -0.5) * (1.0 / math.sqrt(2.0 * math.pi)))
        m = (act * gate).astype(bf16)
        m_ref[:, column : column + HCHUNK] = m
        act_ref[:, column : column + HCHUNK] = act.astype(bf16)
        slope_ref[:, column : column + HCHUNK] = (slope * gate).astype(bf16)
        y = y + dot_nn(m, w_mlp_ref[column : column + HCHUNK, :])
    y_ref[...] = y.astype(bf16)


def middle_back_kernel(
    dy_ref, x1_ref, slope_ref, act_ref, gain_ref, w_out_ref, w_in_ref, w_mlp_ref,
    dh_ref, low_ref, dx1_ref, do_ref, dgain_ref,
):
    dy = dy_ref[...]
    db = None
    for column in range(0, FF, HCHUNK):
        dm = dot_nt(dy, w_mlp_ref[column : column + HCHUNK, :])
        first = (dm * slope_ref[:, column : column + HCHUNK].astype(f32)).astype(bf16)
        second = (dm * act_ref[:, column : column + HCHUNK].astype(f32)).astype(bf16)
        dh_ref[:, column : column + HCHUNK] = first
        dh_ref[:, FF + column : FF + column + HCHUNK] = second
        part = dot_nt(first, w_in_ref[:, column : column + HCHUNK]) + dot_nt(
            second, w_in_ref[:, FF + column : FF + column + HCHUNK]
        )
        db = part if db is None else db + part
    unit, scale = normalize(x1_ref[...])
    back, terms = norm_back(unit, scale, gain_ref[...], db)

    @pl.when(pl.program_id(0) == 0)
    def _():
        dgain_ref[...] = jnp.zeros_like(dgain_ref)

    dgain_ref[...] += jnp.sum(terms, axis=0, keepdims=True)
    dx1 = dy.astype(f32) + back
    dx1_ref[...] = dx1
    low = dx1.astype(bf16)
    low_ref[...] = low
    do_ref[...] = dot_nt(low, w_out_ref[...]).astype(bf16)


def attend_back_kernel(
    q_ref, k_ref, v_ref, o_ref, do_ref, p_ref, cos_ref, sin_ref,
    dq_ref, dk_ref, dv_ref, key_sum, value_sum,
):
    k, v = k_ref[...], v_ref[...]
    lane = lax.broadcasted_iota(jnp.int32, (1, PAIR), 1)
    length = k.shape[0]
    zero = jnp.zeros((), bf16)
    cosine, sine = cos_ref[...], sin_ref[...]
    for tile in range(0, length, TILE):
        rows = slice(tile, tile + TILE)
        q, do = q_ref[rows, :], do_ref[rows, :]
        inner = do.astype(f32) * o_ref[rows, :].astype(f32)
        dq = None
        for head in range(2):
            mine = (lane < HDIM) if head == 0 else (lane >= HDIM)
            do_head = jnp.where(mine, do, zero)
            delta = jnp.sum(jnp.where(mine, inner, 0.0), axis=-1, keepdims=True)
            probs = p_ref[head, rows, :]
            dp = dot_nt(do_head, v)
            ds = (probs.astype(f32) * (dp - delta)).astype(bf16)
            value_part = dot_tn(probs, do_head)
            key_part = dot_tn(ds, jnp.where(mine, q, zero))
            if tile == 0 and head == 0:
                value_sum[...] = value_part
                key_sum[...] = key_part
            else:
                value_sum[...] += value_part
                key_sum[...] += key_part
            part = dot_nn(ds, jnp.where(mine, k, zero))
            dq = part if dq is None else dq + part
        dq = rotate_pair(dq * HDIM**-0.5, cosine[rows], -sine[rows])
        dq_ref[rows, :] = dq.astype(bf16)
    dk_ref[...] = rotate_pair(key_sum[...], cosine, -sine).astype(bf16)
    dv_ref[...] = value_sum[...].astype(bf16)


def last_kernel(dq_ref, dk_ref, dv_ref, x_ref, dx1_ref, gain_ref, w_ref, dx_ref, dgain_ref):
    da = dot_nt(dq_ref[...], w_ref[:, :D])
    da = da + dot_nt(dk_ref[...], w_ref[:, D : 2 * D])
    da = da + dot_nt(dv_ref[...], w_ref[:, 2 * D :])
    unit, scale = normalize(x_ref[...].astype(f32))
    back, terms = norm_back(unit, scale, gain_ref[...], da)

    @pl.when(pl.program_id(0) == 0)
    def _():
        dgain_ref[...] = jnp.zeros_like(dgain_ref)

    dgain_ref[...] += jnp.sum(terms, axis=0, keepdims=True)
    dx_ref[...] = (dx1_ref[...] + back).astype(bf16)


def rows_spec(width):
    return pl.BlockSpec((TILE, width), lambda i: (i, 0))


def whole_spec(*shape):
    return pl.BlockSpec(shape, lambda i: (0,) * len(shape))


def pair_spec(length, offset=0):
    return pl.BlockSpec((length, PAIR), lambda i: (0, i + offset))


def struct(dtype, *shape):
    return jax.ShapeDtypeStruct(shape, dtype)


def call(kernel, grid, in_specs, out_specs, out_shape, flops, scratch=()):
    return pl.pallas_call(
        kernel,
        grid=(grid,),
        in_specs=in_specs,
        out_specs=out_specs,
        out_shape=out_shape,
        scratch_shapes=list(scratch),
        compiler_params=pltpu.CompilerParams(
            dimension_semantics=("arbitrary",), vmem_limit_bytes=VMEM_LIMIT
        ),
        cost_estimate=pl.CostEstimate(flops=flops, bytes_accessed=10 * 2**20, transcendentals=0),
    )


def exchange(array, axis, mask, size):
    return lax.ppermute(array, axis, [(i, i ^ mask) for i in range(size)])


def take(array, index):
    return lax.dynamic_index_in_dim(array, index, 0, keepdims=False)


def swap_blocks(blocks, me, size):
    received = [take(blocks, me)]
    for k in range(1, size):
        received.append(exchange(take(blocks, me ^ k), "seq", k, size))
    return received


def swap_back(slots, me, size):
    arrived = jnp.stack(
        [slots[0]] + [exchange(slots[k], "seq", k, size) for k in range(1, size)]
    )
    return jnp.stack([take(arrived, me ^ s) for s in range(size)])


def gather_weight(shard, me, size):
    parts = shard[None]
    bit = size // 2
    while bit:
        parts = jnp.concatenate([parts, exchange(parts, "fsdp", bit, size)], 0)
        bit //= 2
    order = [0]
    bit = size // 2
    while bit:
        order = order + [o ^ bit for o in order]
        bit //= 2
    back = [order.index(j) for j in range(size)]
    relative = [parts[back[j]] for j in range(size)]
    stacked = jnp.stack(relative)
    ordered = jnp.stack([take(stacked, me ^ j) for j in range(size)])
    return ordered.reshape((size * shard.shape[0],) + shard.shape[1:])


def add_low(left, right):
    return (left.astype(f32) + right.astype(f32)).astype(bf16)


def reduce_packed(packed, sizes):
    fsdp, rep, seq = sizes
    me = lax.axis_index("fsdp")
    array = jnp.stack([take(packed, me ^ j) for j in range(fsdp)])
    bit = 1
    while bit < fsdp:
        halves = array.reshape((array.shape[0] // 2, 2) + array.shape[1:])
        array = add_low(halves[:, 0], exchange(halves[:, 1], "fsdp", bit, fsdp))
        bit *= 2
    array = array[0]
    steps = []
    for axis, size in (("rep", rep), ("seq", seq)):
        bit = 1
        while bit < size:
            steps.append((axis, bit, size))
            bit *= 2
    for axis, bit, size in steps:
        mine = (lax.axis_index(axis) // bit) % 2
        halves = array.reshape(2, array.shape[0] // 2, array.shape[1])
        array = add_low(take(halves, mine), exchange(take(halves, 1 - mine), axis, bit, size))
    for axis, bit, size in reversed(steps):
        mine = (lax.axis_index(axis) // bit) % 2
        other = exchange(array, axis, bit, size)
        first = jnp.where(mine == 0, array, other)
        second = jnp.where(mine == 0, other, array)
        array = jnp.concatenate([first, second], 0)
    return array


def padded_rows(rows, align):
    return -(-rows // align) * align


def body(sizes, tokens, segments, positions, gain_attn, w_qkv, w_out, gain_mlp, w_in, w_mlp_out, cotangent):
    fsdp, rep, seq = sizes
    micro, batch, rows, _ = tokens.shape
    assert micro * batch == seq and rows % TILE == 0
    length = seq * rows
    me_seq, me_fsdp = lax.axis_index("seq"), lax.axis_index("fsdp")

    x_slots = swap_blocks(tokens.reshape(seq, rows, D), me_seq, seq)
    x = jnp.concatenate(x_slots, 0)

    marks = take(segments.reshape(seq, length), me_seq)
    place = jnp.arange(length, dtype=jnp.int32) - jnp.sum(
        (marks[None, :] < marks[:, None]).astype(jnp.int32), axis=1
    )
    slot_order = [me_seq ^ k for k in range(seq)]
    marks = jnp.concatenate([take(marks.reshape(seq, rows), s) for s in slot_order])
    place = jnp.concatenate([take(place.reshape(seq, rows), s) for s in slot_order])
    half = jnp.arange(0, HDIM, 2).astype(f32) / HDIM
    angles = place.astype(f32)[:, None] * jnp.exp(-half * math.log(THETA))
    cosine, sine = jnp.cos(angles), jnp.sin(angles)
    cosine = jnp.concatenate([cosine] * 4, -1)
    sine = jnp.concatenate([-sine, sine] * 2, -1)

    gather = lambda shard: gather_weight(shard, me_fsdp, fsdp)
    gains = gather(jnp.stack([gain_attn, gain_mlp], 1)).astype(f32)
    gain_one, gain_two = gains[:, 0][None], gains[:, 1][None]
    wq = gather(w_qkv)

    tiles, pairs = length // TILE, HEADS // 2
    a, qkv = call(
        first_kernel, tiles,
        [rows_spec(D), whole_spec(1, D), whole_spec(D, 3 * D), rows_spec(PAIR), rows_spec(PAIR)],
        [rows_spec(D), rows_spec(3 * D)],
        [struct(bf16, length, D), struct(bf16, length, 3 * D)],
        2 * length * D * 3 * D,
    )(x, gain_one, wq, cosine, sine)

    prob_spec = pl.BlockSpec((2, length, length), lambda i: (i, 0, 0))
    o, probs = call(
        attend_kernel, pairs,
        [pair_spec(length), pair_spec(length, pairs), pair_spec(length, 2 * pairs),
         whole_spec(length, 1), whole_spec(1, length)],
        [pair_spec(length), prob_spec],
        [struct(bf16, length, D), struct(bf16, HEADS, length, length)],
        16 * length * length * D,
    )(qkv, qkv, qkv, marks[:, None], marks[None, :])

    wo, wi, wm = gather(w_out), gather(w_in), gather(w_mlp_out)
    x1, b, m, slope, act, y = call(
        middle_kernel, tiles,
        [rows_spec(D), rows_spec(D), whole_spec(1, D), whole_spec(D, D), whole_spec(D, 2 * FF), whole_spec(FF, D)],
        [rows_spec(D), rows_spec(D), rows_spec(FF), rows_spec(FF), rows_spec(FF), rows_spec(D)],
        [struct(f32, length, D), struct(bf16, length, D), struct(bf16, length, FF),
         struct(bf16, length, FF), struct(bf16, length, FF), struct(bf16, length, D)],
        2 * length * (D * D + 3 * D * FF),
    )(o, x, gain_two, wo, wi, wm)
    block_out = swap_back([y[k * rows : (k + 1) * rows] for k in range(seq)], me_seq, seq)

    dy = jnp.concatenate(swap_blocks(cotangent.reshape(seq, rows, D), me_seq, seq), 0)
    dh, low, dx1, do, dgain_two = call(
        middle_back_kernel, tiles,
        [rows_spec(D), rows_spec(D), rows_spec(FF), rows_spec(FF), whole_spec(1, D),
         whole_spec(D, D), whole_spec(D, 2 * FF), whole_spec(FF, D)],
        [rows_spec(2 * FF), rows_spec(D), rows_spec(D), rows_spec(D), whole_spec(1, D)],
        [struct(bf16, length, 2 * FF), struct(bf16, length, D), struct(f32, length, D),
         struct(bf16, length, D), struct(f32, 1, D)],
        2 * length * (D * D + 3 * D * FF),
    )(dy, x1, slope, act, gain_two, wo, wi, wm)

    grad_mlp = dot_tn(m, dy).astype(bf16).reshape(fsdp, FF // fsdp, D)
    grad_in = dot_tn(b, dh).astype(bf16).reshape(fsdp, D // fsdp, 3, D).swapaxes(1, 2).reshape(fsdp, 3 * D // fsdp, D)
    grad_out = dot_tn(o, low).astype(bf16).reshape(fsdp, D // fsdp, D)
    parts = [grad_out, grad_mlp, grad_in]
    used = sum(part.shape[1] for part in parts)
    align = 8 * rep * seq
    spare = padded_rows(used, align) - used
    if spare:
        parts.append(jnp.zeros((fsdp, spare, D), bf16))
    reduced = reduce_packed(jnp.concatenate(parts, 1), sizes)

    dq, dk, dv = call(
        attend_back_kernel, pairs,
        [pair_spec(length), pair_spec(length, pairs), pair_spec(length, 2 * pairs),
         pair_spec(length), pair_spec(length), prob_spec, whole_spec(length, PAIR), whole_spec(length, PAIR)],
        [pair_spec(length)] * 3,
        [struct(bf16, length, D)] * 3,
        32 * length * length * D,
        [pltpu.VMEM((length, PAIR), f32)] * 2,
    )(qkv, qkv, qkv, o, do, probs, cosine, sine)

    dx, dgain_one = call(
        last_kernel, tiles,
        [rows_spec(D)] * 5 + [whole_spec(1, D), whole_spec(D, 3 * D)],
        [rows_spec(D), whole_spec(1, D)],
        [struct(bf16, length, D), struct(f32, 1, D)],
        2 * length * D * 3 * D,
    )(dq, dk, dv, x, dx1, gain_one, wq)
    input_grad = swap_back([dx[k * rows : (k + 1) * rows] for k in range(seq)], me_seq, seq)

    grad_qkv = dot_tn(a, jnp.concatenate([dq, dk, dv], 1)).astype(bf16).reshape(fsdp, D // fsdp, 3 * D)
    spare = padded_rows(D // fsdp, align) - D // fsdp
    if spare:
        grad_qkv = jnp.pad(grad_qkv, ((0, 0), (0, spare), (0, 0)))
    qkv_reduced = reduce_packed(grad_qkv, sizes)[: D // fsdp].astype(f32)

    dgains = jnp.concatenate([dgain_one, dgain_two], 0)
    for axis, size in (("fsdp", fsdp), ("rep", rep), ("seq", seq)):
        bit = 1
        while bit < size:
            dgains = dgains + exchange(dgains, axis, bit, size)
            bit *= 2
    dgains = lax.dynamic_slice_in_dim(dgains, me_fsdp * (D // fsdp), D // fsdp, 1)

    first = D // fsdp
    second = first + FF // fsdp
    third = second + 3 * D // fsdp
    full = reduced.astype(f32)
    return (
        block_out.reshape(tokens.shape),
        input_grad.astype(f32).reshape(tokens.shape),
        dgains[0],
        qkv_reduced,
        full[:first],
        dgains[1],
        full[second:third].reshape(3, D // fsdp, D).swapaxes(0, 1).reshape(D // fsdp, 3 * D),
        full[first:second],
    )


def solution(mesh):
    sizes = (mesh.shape["fsdp"], mesh.shape["rep"], mesh.shape["seq"])
    wide = P(None, ("rep", "fsdp"), "seq", None)
    placed = (
        wide, P(None, ("rep", "fsdp"), None), P(None, ("rep", "fsdp"), "seq"),
        P("fsdp"), P("fsdp", None), P("fsdp", None), P("fsdp"), P("fsdp", None), P("fsdp", None), wide,
    )
    return jax.shard_map(
        functools.partial(body, sizes),
        mesh=mesh,
        in_specs=placed,
        out_specs=(
            wide, wide, P("fsdp"), P("fsdp", None), P("fsdp", None), P("fsdp"), P("fsdp", None), P("fsdp", None),
        ),
        check_vma=False,
    )
```

time: 1290 us -> 420 us (0.33)
  waiting for transfers between devices: 657 us -> 149 us
  matrix products: 257 us -> 17.4 us
  local copies, waits for them, and re-layouts: 219 us -> 33.7 us
  Pallas kernels: 0 us -> 123 us
  other arithmetic: 94.1 us -> 38.9 us
  starting transfers between devices: 2.02 us -> 49.5 us
  blocking collectives: 37.9 us -> 0 us
  between operations: 17.3 us -> 1.74 us
    reduce_scatter x12 -> x0, waiting for transfers between devices: 351 us -> none  [the longest x2 86.1 us: body(): lax.psum_scatter(grads[1].astype(jnp.bfloat16), 'fsdp', scatter_dimension...]
    dot_general x66 -> x4, matrix products: 257 us -> 17.4 us  [dot_tn(): lax.dot_general(left, right, (((0,), (0,)), ((), ())), preferred_element_...]
    all_gather x8 -> x0, waiting for transfers between devices: 167 us -> none  [the longest x2 119 us: body(): lax.all_gather(value, 'seq', axis=1, tiled=True)]
    ppermute x0 -> x43, waiting for transfers between devices: none -> 149 us  [exchange(): return lax.ppermute(array, axis, [(i, i ^ mask) for i in range(size)])]
    psum x1 -> x0, waiting for transfers between devices: 135 us -> none  [body(): lax.psum(lax.psum_scatter(grads[1].astype(jnp.bfloat16), 'fsdp', scatter_...]
    pallas_call x0 -> x6, Pallas kernels: none -> 123 us  [the longest x1 34.7 us: body(): call(attend_back_kernel, pairs, [pair_spec(length), pair_spec(length, pai...]
    ppermute x0 -> x43, starting transfers between devices: none -> 49.5 us  [exchange(): return lax.ppermute(array, axis, [(i, i ^ mask) for i in range(size)])]
    dynamic_update_slice x30 -> x0, local copies, waits for them, and re-layouts: 49.4 us -> none  [the longest x12 31.2 us: one(): lax.dynamic_update_slice_in_dim(grad_v, value_part.reshape(batch, length,...]
  transfers between devices with their start and end apart: 21 -> 43, of which waited for: 17 -> 21; matrix products, arithmetic and copies ran while one was open for 28% -> 17% of each run, Pallas kernels for 0% -> 15%
where the time goes in v1:
time: 420 us; the launch traced here: 413 us
  waiting for transfers between devices  149 us (35%)
  Pallas kernels  123 us (29%)
  starting transfers between devices  49.5 us (12%)
  other arithmetic  38.9 us (9%)
  local copies, waits for them, and re-layouts  33.7 us (8%)
  matrix products  17.4 us (4%)
    ppermute x43, waiting for transfers between devices, exchange(): return lax.ppermute(array, axis, [(i, i ^ mask) for i in range(size)])  149 us
    ppermute x43, starting transfers between devices, exchange(): return lax.ppermute(array, axis, [(i, i ^ mask) for i in range(size)])  49.5 us
    pallas_call x1, Pallas kernels, body(): call(attend_back_kernel, pairs, [pair_spec(length), pair_spec(length, pai...  34.7 us
    pallas_call x1, Pallas kernels, body(): call(attend_kernel, pairs, [pair_spec(length), pair_spec(length, pairs),...  33.7 us
    pallas_call x1, Pallas kernels, body(): call(middle_back_kernel, tiles, [rows_spec(D), rows_spec(D), rows_spec(FF...  18.1 us
    dot_general x4, matrix products, dot_tn(): lax.dot_general(left, right, (((0,), (0,)), ((), ())), preferred_element_...  17.4 us
    pallas_call x1, Pallas kernels, body(): call(middle_kernel, tiles, [rows_spec(D), rows_spec(D), whole_spec(1, D),...  17.2 us
    pallas_call x1, Pallas kernels, body(): call(last_kernel, tiles, [rows_spec(D)] * 5 + [whole_spec(1, D), whole_sp...  10.1 us
  transfers between devices with their start and end apart: 43, of which 21 were waited for; matrix products, arithmetic and copies ran while one was open for 17% of the time, Pallas kernels for 15%

profile of v1, /device:TPU:0, one launch (start us, length us, event | category | flops | bytes accessed | tf_op | source)
XLA Modules:
  0.0 413.1 jit_solution(9718845580190334517)
XLA Ops:
  31.6 23.3 %collective-permute-done.1 = bf16[256,768]{1,0:T(8,128)(2,1)} collective-permute-done((bf16[256,768]{1,0:T(8,128)(2,1)}, bf16[256,768]{1,0:T(8,128)(2,1)}, u32[]{:S(2)}, u32[]{:S(2)}) %collective-permute-start.1) | collective-permute-done | bytes 393248 | tf_op jit(solution)/shard_map/ppermute | solution.py:247
  54.9 9.7 %collective-permute-start.16 = (bf16[256,768]{1,0:T(8,128)(2,1)}, bf16[256,768]{1,0:T(8,128)(2,1)S(1)}, u32[]{:S(2)}, u32[]{:S(2)}) collective-permute-start(bf16[256,768]{1,0:T(8,128)(2,1)} %get-tuple-element.87), channel_id=1, source_target_pairs={{0,1},{1,0},{2,3},{3,2},{4,5},{5,4},{6,7},{7,6},{8,9},{9,8},{10,11... | collective-permute-start | bytes 1179656 | tf_op jit(solution)/shard_map/ppermute | solution.py:247
  70.4 8.7 %collective-permute-done.17 = bf16[256,768]{1,0:T(8,128)(2,1)S(1)} collective-permute-done((bf16[256,768]{1,0:T(8,128)(2,1)}, bf16[256,768]{1,0:T(8,128)(2,1)S(1)}, u32[]{:S(2)}, u32[]{:S(2)}) %collective-permute-start.17) | collective-permute-done | bytes 393248 | tf_op jit(solution)/shard_map/ppermute | solution.py:247
  93.1 9.1 %shard_map.152 = (bf16[1024,768]{1,0:T(8,128)(2,1)}, bf16[1024,2304]{1,0:T(8,128)(2,1)}) custom-call(bf16[1024,768]{1,0:T(8,128)(2,1)} %pad_maximum_fusion.10.x_ref, f32[1,768]{1,0:T(1,128)} %get-tuple-element.119.gain_ref, bf16[768,2304]{1,0:T(8,128)(2,1)} %bitcast.166, f32[1024,128]{1,0:T(8,128)} %pad_maximum_fusion.21.cos_ref, ...), custom_call_target="tpu_custom_call" | custom-call | flops 3623878656 | bytes 10485760 | tf_op jit(solution)/shard_map/pallas_call | solution.py:352
  102.2 33.7 %shard_map.153 = (bf16[1024,768]{1,0:T(8,128)(2,1)}, bf16[12,1024,1024]{2,1,0:T(8,128)(2,1)}) custom-call(bf16[1024,2304]{1,0:T(8,128)(2,1)} %get-tuple-element.28.q_ref.k_ref.v_ref, bf16[1024,2304]{1,0:T(8,128)(2,1)} %get-tuple-element.28.q_ref.k_ref.v_ref, bf16[1024,2304]{1,0:T(8,128)(2,1)} %get-tuple-element.28.q_ref.k_ref.v_ref, ...), custom_call_target="tpu_custom_call" | custom-call | flops 12884901888 | bytes 10485760 | tf_op jit(solution)/shard_map/pallas_call | solution.py:361
  137.9 17.2 %shard_map.154 = (f32[1024,768]{1,0:T(8,128)}, bf16[1024,768]{1,0:T(8,128)(2,1)}, bf16[1024,1152]{1,0:T(8,128)(2,1)}, bf16[1024,1152]{1,0:T(8,128)(2,1)}, bf16[1...) custom-call(bf16[1024,768]{1,0:T(8,128)(2,1)} %get-tuple-element.29.o_ref, bf16[1024,768]{1,0:T(8,128)(2,1)} %pad_maximum_fusion.10.x_ref, ...), custom_call_target="tpu_custom_call" | custom-call | flops 6643777536 | bytes 10485760 | tf_op jit(solution)/shard_map/pallas_call | solution.py:371
  160.2 4.4 %collective-permute-start.14 = (bf16[256,768]{1,0:T(8,128)(2,1)}, bf16[256,768]{1,0:T(8,128)(2,1)}, u32[]{:S(2)}, u32[]{:S(2)}) collective-permute-start(bf16[256,768]{1,0:T(8,128)(2,1)} %get-tuple-element.94), channel_id=1, source_target_pairs={{0,2},{1,3},{2,0},{3,1},{4,6},{5,7},{6,4},{7,5},{8,10},{9,11},{10,... | collective-permute-start | bytes 1179656 | tf_op jit(solution)/shard_map/ppermute | solution.py:247
  164.6 18.1 %shard_map.155 = (bf16[1024,2304]{1,0:T(8,128)(2,1)}, bf16[1024,768]{1,0:T(8,128)(2,1)}, f32[1024,768]{1,0:T(8,128)}, bf16[1024,768]{1,0:T(8,128)(2,1)}, f32[1,768]{1,0:T(1,128)}) custom-call(bf16[1024,768]{1,0:T(8,128)(2,1)} %pad_maximum_fusion.13.dy_ref, f32[1024,768]{1,0:T(8,128)} %get-tuple-element.31.x1_ref, ...), custom_call_target="tpu_custom_call" | custom-call | flops 6643777536 | bytes 10485760 | tf_op jit(solution)/shard_map/pallas_call | solution.py:382
  186.6 34.7 %shard_map.156 = (bf16[1024,768]{1,0:T(8,128)(2,1)}, bf16[1024,768]{1,0:T(8,128)(2,1)}, bf16[1024,768]{1,0:T(8,128)(2,1)}) custom-call(bf16[1024,2304]{1,0:T(8,128)(2,1)} %get-tuple-element.28.q_ref.k_ref.v_ref, bf16[1024,2304]{1,0:T(8,128)(2,1)} %get-tuple-element.28.q_ref.k_ref.v_ref, bf16[1024,2304]{1,0:T(8,128)(2,1)} %get-tuple-element.28.q_ref.k_ref.v_ref, ...), custom_call_target="tpu_custom_call" | custom-call | flops 25769803776 | bytes 10485760 | tf_op jit(solution)/shard_map/pallas_call | solution.py:403
  221.4 10.1 %shard_map.157 = (bf16[1024,768]{1,0:T(8,128)(2,1)}, f32[1,768]{1,0:T(1,128)}) custom-call(bf16[1024,768]{1,0:T(8,128)(2,1)} %get-tuple-element.36.dq_ref, bf16[1024,768]{1,0:T(8,128)(2,1)} %get-tuple-element.37.dk_ref, bf16[1024,768]{1,0:T(8,128)(2,1)} %get-tuple-element.38.dv_ref, bf16[1024,768]{1,0:T(8,128)(2,1)} %pad_maximum_fusion.10.x_ref, ...), custom_call_target="tpu_custom_call" | custom-call | flops 3623878656 | bytes 10485760 | tf_op jit(solution)/shard_map/pallas_call | solution.py:413
  231.5 4.9 %convolution_convert_fusion.1 = bf16[768,2304]{1,0:T(8,128)(2,1)S(1)} fusion(bf16[1024,768]{1,0:T(8,128)(2,1)S(1)} %copy-done.29, bf16[1024,768]{1,0:T(8,128)(2,1)S(1)} %copy-done.25, bf16[1024,768]{1,0:T(8,128)(2,1)S(1)} %copy-done.24, bf16[1024,768]{1,0:T(8,128)(2,1)S(1)} %copy-done.23), kind=kOutput, calls=%fused_computation.5 | convolution fusion | flops 3639803904 | bytes 9830400 | tf_op jit(solution)/shard_map/dot_general | solution.py:35
  240.5 5.4 %convolution_convert_fusion = bf16[768,2304]{1,0:T(8,128)(2,1)} fusion(bf16[1024,768]{1,0:T(8,128)(2,1)S(1)} %copy-done.27, bf16[1024,2304]{1,0:T(8,128)(2,1)S(1)} %bitcast.215), kind=kOutput, calls=%fused_computation.4 | convolution fusion | flops 3625648128 | bytes 9830400 | tf_op jit(solution)/shard_map/dot_general | solution.py:35
  245.9 8.7 %reshape.209 = bf16[4,192,3,768]{3,2,1,0:T(4,128)(2,1)} reshape(bf16[768,2304]{1,0:T(8,128)(2,1)} %convolution_convert_fusion) | data formatting | bytes 7077888 | tf_op jit(solution)/shard_map/reshape | solution.py:393
  283.0 12.8 %collective-permute-done.13 = bf16[256,768]{1,0:T(8,128)(2,1)S(1)} collective-permute-done((bf16[256,768]{1,0:T(8,128)(2,1)S(1)}, bf16[256,768]{1,0:T(8,128)(2,1)S(1)}, u32[]{:S(2)}, u32[]{:S(2)}) %collective-permute-start.13) | collective-permute-done | bytes 393248 | tf_op jit(solution)/shard_map/ppermute | solution.py:247
  302.5 5.7 %collective-permute-done.29 = bf16[96,2304]{1,0:T(8,128)(2,1)S(1)} collective-permute-done((bf16[96,2304]{1,0:T(8,128)(2,1)S(1)}, bf16[96,2304]{1,0:T(8,128)(2,1)S(1)}, u32[]{:S(2)}, u32[]{:S(2)}) %collective-permute-start.29) | collective-permute-done | bytes 442400 | tf_op jit(solution)/shard_map/ppermute | solution.py:247
  308.4 7.4 %collective-permute-done.20 = bf16[256,768]{1,0:T(8,128)(2,1)S(1)} collective-permute-done((bf16[256,768]{1,0:T(8,128)(2,1)S(1)}, bf16[256,768]{1,0:T(8,128)(2,1)S(1)}, u32[]{:S(2)}, u32[]{:S(2)}) %collective-permute-start.20) | collective-permute-done | bytes 393248 | tf_op jit(solution)/shard_map/ppermute | solution.py:247
  319.5 17.3 %collective-permute-done.36 = bf16[1,1088,768]{2,1,0:T(8,128)(2,1)S(1)} collective-permute-done((bf16[1,1088,768]{2,1,0:T(8,128)(2,1)S(1)}, bf16[1,1088,768]{2,1,0:T(8,128)(2,1)S(1)}, u32[]{:S(2)}, u32[]{:S(2)}) %collective-permute-start.36) | collective-permute-done | bytes 1671200 | tf_op jit(solution)/shard_map/ppermute | solution.py:247
  339.4 5.2 %collective-permute-done.31 = bf16[24,2304]{1,0:T(8,128)(2,1)S(1)} collective-permute-done((bf16[24,2304]{1,0:T(8,128)(2,1)S(1)}, bf16[24,2304]{1,0:T(8,128)(2,1)S(1)}, u32[]{:S(2)}, u32[]{:S(2)}) %collective-permute-start.31) | collective-permute-done | bytes 110624 | tf_op jit(solution)/shard_map/ppermute | solution.py:247
  344.6 10.1 %collective-permute-done.37 = bf16[544,768]{1,0:T(8,128)(2,1)S(1)} collective-permute-done((bf16[544,768]{1,0:T(8,128)(2,1)S(1)}, bf16[544,768]{1,0:T(8,128)(2,1)S(1)}, u32[]{:S(2)}, u32[]{:S(2)}) %collective-permute-start.37) | collective-permute-done | bytes 835616 | tf_op jit(solution)/shard_map/ppermute | solution.py:247
  355.1 12.5 %collective-permute-done.38 = bf16[272,768]{1,0:T(8,128)(2,1)S(1)} collective-permute-done((bf16[272,768]{1,0:T(8,128)(2,1)S(1)}, bf16[272,768]{1,0:T(8,128)(2,1)S(1)}, u32[]{:S(2)}, u32[]{:S(2)}) %collective-permute-start.38) | collective-permute-done | bytes 417824 | tf_op jit(solution)/shard_map/ppermute | solution.py:247
  367.9 8.3 %collective-permute-done.39 = bf16[136,768]{1,0:T(8,128)(2,1)S(1)} collective-permute-done((bf16[136,768]{1,0:T(8,128)(2,1)S(1)}, bf16[136,768]{1,0:T(8,128)(2,1)S(1)}, u32[]{:S(2)}, u32[]{:S(2)}) %collective-permute-start.39) | collective-permute-done | bytes 208928 | tf_op jit(solution)/shard_map/ppermute | solution.py:247
  376.4 8.0 %collective-permute-done.40 = bf16[136,768]{1,0:T(8,128)(2,1)S(1)} collective-permute-done((bf16[136,768]{1,0:T(8,128)(2,1)S(1)}, bf16[136,768]{1,0:T(8,128)(2,1)S(1)}, u32[]{:S(2)}, u32[]{:S(2)}) %collective-permute-start.40) | collective-permute-done | bytes 208928 | tf_op jit(solution)/shard_map/ppermute | solution.py:247
  387.4 5.3 %collective-permute-done.41 = bf16[272,768]{1,0:T(8,128)(2,1)S(1)} collective-permute-done((bf16[272,768]{1,0:T(8,128)(2,1)S(1)}, bf16[272,768]{1,0:T(8,128)(2,1)S(1)}, u32[]{:S(2)}, u32[]{:S(2)}) %collective-permute-start.41) | collective-permute-done | bytes 417824 | tf_op jit(solution)/shard_map/ppermute | solution.py:247
  399.3 8.3 %collective-permute-done.42 = bf16[544,768]{1,0:T(8,128)(2,1)S(1)} collective-permute-done((bf16[544,768]{1,0:T(8,128)(2,1)S(1)}, bf16[544,768]{1,0:T(8,128)(2,1)S(1)}, u32[]{:S(2)}, u32[]{:S(2)}) %collective-permute-start.42) | collective-permute-done | bytes 835616 | tf_op jit(solution)/shard_map/ppermute | solution.py:247
  (248 shorter events, 122.5 us)
Async XLA Ops:
  2.6 19.1 %collective-permute-start.3 = (bf16[1,192,2]{1,0,2:T(2,128)(2,1)}, bf16[1,192,2]{1,0,2:T(2,128)(2,1)}, u32[]{:S(2)}, u32[]{:S(2)}) collective-permute-start(bf16[1,192,2]{1,0,2:T(2,128)(2,1)} %copy.44), channel_id=1, source_target_pairs={{0,8},{4,12},{8,0},{12,4},{1,9},{5,13},{9,1},{13,5},{2,10},{6,14},... | collective-permute-start | bytes 2312 | tf_op jit(solution)/shard_map/ppermute | solution.py:247
  5.5 23.2 %collective-permute-start.7 = (bf16[1,192,768]{2,1,0:T(8,128)(2,1)}, bf16[1,192,768]{2,1,0:T(8,128)(2,1)S(1)}, u32[]{:S(2)}, u32[]{:S(2)}) collective-permute-start(bf16[1,192,768]{2,1,0:T(8,128)(2,1)} %bitcast.190), channel_id=1, source_target_pairs={{0,8},{4,12},{8,0},{12,4},{1,9},{5,13},{9,1},{13,5},{2,10},{6,14},... | collective-permute-start | bytes 884744 | tf_op jit(solution)/shard_map/ppermute | solution.py:247
  8.1 23.0 %collective-permute-start.2 = (bf16[256,768]{1,0:T(8,128)(2,1)}, bf16[256,768]{1,0:T(8,128)(2,1)}, u32[]{:S(2)}, u32[]{:S(2)}) collective-permute-start(bf16[256,768]{1,0:T(8,128)(2,1)} %get-tuple-element.97), channel_id=1, source_target_pairs={{0,3},{1,2},{2,1},{3,0},{4,7},{5,6},{6,5},{7,4},{8,11},{9,10},{10,... | collective-permute-start | bytes 1179656 | tf_op jit(solution)/shard_map/ppermute | solution.py:247
  12.2 42.7 %collective-permute-start.1 = (bf16[256,768]{1,0:T(8,128)(2,1)}, bf16[256,768]{1,0:T(8,128)(2,1)}, u32[]{:S(2)}, u32[]{:S(2)}) collective-permute-start(bf16[256,768]{1,0:T(8,128)(2,1)} %get-tuple-element.98), channel_id=1, source_target_pairs={{0,2},{1,3},{2,0},{3,1},{4,6},{5,7},{6,4},{7,5},{8,10},{9,11},{10,... | collective-permute-start | bytes 1179656 | tf_op jit(solution)/shard_map/ppermute | solution.py:247
  12.2 42.7 %collective-permute-start = (bf16[256,768]{1,0:T(8,128)(2,1)}, bf16[256,768]{1,0:T(8,128)(2,1)}, u32[]{:S(2)}, u32[]{:S(2)}) collective-permute-start(bf16[256,768]{1,0:T(8,128)(2,1)} %get-tuple-element.99), channel_id=1, source_target_pairs={{0,1},{1,0},{2,3},{3,2},{4,5},{5,4},{6,7},{7,6},{8,9},{9,8},{10,11... | collective-permute-start | bytes 1179656 | tf_op jit(solution)/shard_map/ppermute | solution.py:247
  24.2 41.0 %collective-permute-start.18 = (bf16[256,768]{1,0:T(8,128)(2,1)}, bf16[256,768]{1,0:T(8,128)(2,1)}, u32[]{:S(2)}, u32[]{:S(2)}) collective-permute-start(bf16[256,768]{1,0:T(8,128)(2,1)} %get-tuple-element.85), channel_id=1, source_target_pairs={{0,3},{1,2},{2,1},{3,0},{4,7},{5,6},{6,5},{7,4},{8,11},{9,10},{10,... | collective-permute-start | bytes 1179656 | tf_op jit(solution)/shard_map/ppermute | solution.py:247
  29.4 52.7 %collective-permute-start.5 = (bf16[1,192,2304]{2,1,0:T(8,128)(2,1)S(1)}, bf16[1,192,2304]{2,1,0:T(8,128)(2,1)S(1)}, u32[]{:S(2)}, u32[]{:S(2)}) collective-permute-start(bf16[1,192,2304]{2,1,0:T(8,128)(2,1)S(1)} %bitcast.160), channel_id=1, source_target_pairs={{0,8},{4,12},{8,0},{12,4},{1,9},{5,13},{9,1},{13,5},{2,10},{6,14},... | collective-permute-start | bytes 2654216 | tf_op jit(solution)/shard_map/ppermute | solution.py:247
  31.1 50.5 %collective-permute-start.11 = (bf16[1,288,768]{2,1,0:T(8,128)(2,1)S(1)}, bf16[1,288,768]{2,1,0:T(8,128)(2,1)S(1)}, u32[]{:S(2)}, u32[]{:S(2)}) collective-permute-start(bf16[1,288,768]{2,1,0:T(8,128)(2,1)S(1)} %bitcast.175), channel_id=1, source_target_pairs={{0,8},{4,12},{8,0},{12,4},{1,9},{5,13},{9,1},{13,5},{2,10},{6,14},... | collective-permute-start | bytes 1327112 | tf_op jit(solution)/shard_map/ppermute | solution.py:247
  54.9 24.2 %collective-permute-start.17 = (bf16[256,768]{1,0:T(8,128)(2,1)}, bf16[256,768]{1,0:T(8,128)(2,1)S(1)}, u32[]{:S(2)}, u32[]{:S(2)}) collective-permute-start(bf16[256,768]{1,0:T(8,128)(2,1)} %get-tuple-element.86), channel_id=1, source_target_pairs={{0,2},{1,3},{2,0},{3,1},{4,6},{5,7},{6,4},{7,5},{8,10},{9,11},{10,... | collective-permute-start | bytes 1179656 | tf_op jit(solution)/shard_map/ppermute | solution.py:247
  54.9 24.2 %collective-permute-start.16 = (bf16[256,768]{1,0:T(8,128)(2,1)}, bf16[256,768]{1,0:T(8,128)(2,1)S(1)}, u32[]{:S(2)}, u32[]{:S(2)}) collective-permute-start(bf16[256,768]{1,0:T(8,128)(2,1)} %get-tuple-element.87), channel_id=1, source_target_pairs={{0,1},{1,0},{2,3},{3,2},{4,5},{5,4},{6,7},{7,6},{8,9},{9,8},{10,11... | collective-permute-start | bytes 1179656 | tf_op jit(solution)/shard_map/ppermute | solution.py:247
  65.2 17.3 %collective-permute-start.9 = (bf16[1,192,2304]{2,1,0:T(8,128)(2,1)S(1)}, bf16[1,192,2304]{2,1,0:T(8,128)(2,1)S(1)}, u32[]{:S(2)}, u32[]{:S(2)}) collective-permute-start(bf16[1,192,2304]{2,1,0:T(8,128)(2,1)S(1)} %bitcast.163), channel_id=1, source_target_pairs={{0,8},{4,12},{8,0},{12,4},{1,9},{5,13},{9,1},{13,5},{2,10},{6,14},... | collective-permute-start | bytes 2654216 | tf_op jit(solution)/shard_map/ppermute | solution.py:247
  157.7 123.8 %collective-permute-start.15 = (bf16[256,768]{1,0:T(8,128)(2,1)}, bf16[256,768]{1,0:T(8,128)(2,1)}, u32[]{:S(2)}, u32[]{:S(2)}) collective-permute-start(bf16[256,768]{1,0:T(8,128)(2,1)} %get-tuple-element.93), channel_id=1, source_target_pairs={{0,3},{1,2},{2,1},{3,0},{4,7},{5,6},{6,5},{7,4},{8,11},{9,10},{10,... | collective-permute-start | bytes 1179656 | tf_op jit(solution)/shard_map/ppermute | solution.py:247
  160.2 122.3 %collective-permute-start.14 = (bf16[256,768]{1,0:T(8,128)(2,1)}, bf16[256,768]{1,0:T(8,128)(2,1)}, u32[]{:S(2)}, u32[]{:S(2)}) collective-permute-start(bf16[256,768]{1,0:T(8,128)(2,1)} %get-tuple-element.94), channel_id=1, source_target_pairs={{0,2},{1,3},{2,0},{3,1},{4,6},{5,7},{6,4},{7,5},{8,10},{9,11},{10,... | collective-permute-start | bytes 1179656 | tf_op jit(solution)/shard_map/ppermute | solution.py:247
  237.8 24.8 %collective-permute-start.22 = (f32[2,768]{1,0:T(2,128)}, f32[2,768]{1,0:T(2,128)S(1)}, u32[]{:S(2)}, u32[]{:S(2)}) collective-permute-start(f32[2,768]{1,0:T(2,128)} %pad_maximum_fusion.26), channel_id=1, source_target_pairs={{0,4},{4,0},{8,12},{12,8},{1,5},{5,1},{9,13},{13,9},{2,6},{6,2},{1... | collective-permute-start | bytes 18440 | tf_op jit(solution)/shard_map/ppermute | solution.py:247
  239.6 35.5 %collective-permute-start.27 = (bf16[2,192,2304]{2,1,0:T(8,128)(2,1)}, bf16[2,192,2304]{2,1,0:T(8,128)(2,1)}, u32[]{:S(2)}, u32[]{:S(2)}) collective-permute-start(bf16[2,192,2304]{2,1,0:T(8,128)(2,1)} %slice_bitcast_fusion.2), channel_id=1, source_target_pairs={{0,4},{4,0},{8,12},{12,8},{1,5},{5,1},{9,13},{13,9},{2,6},{6,2},{1... | collective-permute-start | bytes 5308424 | tf_op jit(solution)/shard_map/ppermute | solution.py:247
  270.8 28.7 %collective-permute-start.35 = (bf16[2,1088,768]{2,1,0:T(8,128)(2,1)S(1)}, bf16[2,1088,768]{2,1,0:T(8,128)(2,1)S(1)}, u32[]{:S(2)}, u32[]{:S(2)}) collective-permute-start(bf16[2,1088,768]{2,1,0:T(8,128)(2,1)S(1)} %slice_bitcast_fusion), channel_id=1, source_target_pairs={{0,4},{4,0},{8,12},{12,8},{1,5},{5,1},{9,13},{13,9},{2,6},{6,2},{1... | collective-permute-start | bytes 10027016 | tf_op jit(solution)/shard_map/ppermute | solution.py:247
  277.1 20.6 %collective-permute-start.28 = (bf16[1,192,2304]{2,1,0:T(8,128)(2,1)S(1)}, bf16[1,192,2304]{2,1,0:T(8,128)(2,1)S(1)}, u32[]{:S(2)}, u32[]{:S(2)}) collective-permute-start(bf16[1,192,2304]{2,1,0:T(8,128)(2,1)S(1)} %slice_bitcast_fusion.6), channel_id=1, source_target_pairs={{0,8},{4,12},{8,0},{12,4},{1,9},{5,13},{9,1},{13,5},{2,10},{6,14},... | collective-permute-start | bytes 2654216 | tf_op jit(solution)/shard_map/ppermute | solution.py:247
  278.7 17.1 %collective-permute-start.13 = (bf16[256,768]{1,0:T(8,128)(2,1)S(1)}, bf16[256,768]{1,0:T(8,128)(2,1)S(1)}, u32[]{:S(2)}, u32[]{:S(2)}) collective-permute-start(bf16[256,768]{1,0:T(8,128)(2,1)S(1)} %copy-done.17), channel_id=1, source_target_pairs={{0,1},{1,0},{2,3},{3,2},{4,5},{5,4},{6,7},{7,6},{8,9},{9,8},{10,11... | collective-permute-start | bytes 1179656 | tf_op jit(solution)/shard_map/ppermute | solution.py:247
  281.5 26.9 %collective-permute-start.21 = (bf16[256,768]{1,0:T(8,128)(2,1)S(1)}, bf16[256,768]{1,0:T(8,128)(2,1)S(1)}, u32[]{:S(2)}, u32[]{:S(2)}) collective-permute-start(bf16[256,768]{1,0:T(8,128)(2,1)S(1)} %get-tuple-element.81), channel_id=1, source_target_pairs={{0,3},{1,2},{2,1},{3,0},{4,7},{5,6},{6,5},{7,4},{8,11},{9,10},{10,... | collective-permute-start | bytes 1179656 | tf_op jit(solution)/shard_map/ppermute | solution.py:247
  282.4 33.3 %collective-permute-start.20 = (bf16[256,768]{1,0:T(8,128)(2,1)S(1)}, bf16[256,768]{1,0:T(8,128)(2,1)S(1)}, u32[]{:S(2)}, u32[]{:S(2)}) collective-permute-start(bf16[256,768]{1,0:T(8,128)(2,1)S(1)} %get-tuple-element.82), channel_id=1, source_target_pairs={{0,2},{1,3},{2,0},{3,1},{4,6},{5,7},{6,4},{7,5},{8,10},{9,11},{10,... | collective-permute-start | bytes 1179656 | tf_op jit(solution)/shard_map/ppermute | solution.py:247
  295.8 19.9 %collective-permute-start.19 = (bf16[256,768]{1,0:T(8,128)(2,1)S(1)}, bf16[256,768]{1,0:T(8,128)(2,1)S(1)}, u32[]{:S(2)}, u32[]{:S(2)}) collective-permute-start(bf16[256,768]{1,0:T(8,128)(2,1)S(1)} %get-tuple-element.83), channel_id=1, source_target_pairs={{0,1},{1,0},{2,3},{3,2},{4,5},{5,4},{6,7},{7,6},{8,9},{9,8},{10,11... | collective-permute-start | bytes 1179656 | tf_op jit(solution)/shard_map/ppermute | solution.py:247
  300.6 36.2 %collective-permute-start.36 = (bf16[1,1088,768]{2,1,0:T(8,128)(2,1)S(1)}, bf16[1,1088,768]{2,1,0:T(8,128)(2,1)S(1)}, u32[]{:S(2)}, u32[]{:S(2)}) collective-permute-start(bf16[1,1088,768]{2,1,0:T(8,128)(2,1)S(1)} %slice_bitcast_fusion.4), channel_id=1, source_target_pairs={{0,8},{4,12},{8,0},{12,4},{1,9},{5,13},{9,1},{13,5},{2,10},{6,14},... | collective-permute-start | bytes 5013512 | tf_op jit(solution)/shard_map/ppermute | solution.py:247
  337.3 17.4 %collective-permute-start.37 = (bf16[544,768]{1,0:T(8,128)(2,1)S(1)}, bf16[544,768]{1,0:T(8,128)(2,1)S(1)}, u32[]{:S(2)}, u32[]{:S(2)}) collective-permute-start(bf16[544,768]{1,0:T(8,128)(2,1)S(1)} %dynamic-slice_bitcast_fusion), channel_id=1, source_target_pairs={{0,16},{16,0},{1,17},{17,1},{2,18},{18,2},{3,19},{19,3},{4,20},{20... | collective-permute-start | bytes 2506760 | tf_op jit(solution)/shard_map/ppermute | solution.py:247
  392.8 14.7 %collective-permute-start.42 = (bf16[544,768]{1,0:T(8,128)(2,1)S(1)}, bf16[544,768]{1,0:T(8,128)(2,1)S(1)}, u32[]{:S(2)}, u32[]{:S(2)}) collective-permute-start(bf16[544,768]{1,0:T(8,128)(2,1)S(1)} %pad_maximum_fusion.19), channel_id=1, source_target_pairs={{0,16},{16,0},{1,17},{17,1},{2,18},{18,2},{3,19},{19,3},{4,20},{20... | collective-permute-start | bytes 2506760 | tf_op jit(solution)/shard_map/ppermute | solution.py:247
  (51 other events, 408.5 us)

commit v2 on v1

--- a/solution.py
+++ b/solution.py
@@ -82,17 +82,35 @@
             qkv_ref[:, start : start + PAIR] = piece.astype(bf16)
 
 
-def attend_kernel(q_ref, k_ref, v_ref, rows_ref, cols_ref, o_ref, p_ref):
+def attend_kernel(
+    sizes, q_ref, k_ref, v_ref, rows_ref, cols_ref, cot_ref, o_ref, p_ref, dy_ref, bounce, *sem_refs
+):
+    seq = sizes[2]
+    step, last = pl.program_id(0), pl.num_programs(0) - 1
+    sems = Sems(*sem_refs)
+    me_seq = lax.axis_index("seq")
+    into = sems.copy(cot_ref.at[me_seq], bounce)
+    outof = sems.copy(bounce, dy_ref.at[0])
+    blocks = [sems.remote(cot_ref.at[flip(me_seq, k)], dy_ref.at[k], "seq", k) for k in range(1, seq)]
+
+    @pl.when(step == 0)
+    def _():
+        into.start()
+        meet([("seq", k) for k in range(1, seq)])
+        start_all(blocks)
+        into.wait()
+        outof.start()
+
     k, v = k_ref[...], v_ref[...]
     lane = lax.broadcasted_iota(jnp.int32, (1, PAIR), 1)
     length = k.shape[0]
+    zero = jnp.zeros((), bf16)
     for tile in range(0, length, TILE):
         q = q_ref[tile : tile + TILE, :]
         same = rows_ref[tile : tile + TILE, :] == cols_ref[...]
         out = None
         for head in range(2):
             mine = (lane < HDIM) if head == 0 else (lane >= HDIM)
-            zero = jnp.zeros((), bf16)
             scores = dot_nt(jnp.where(mine, q, zero), k)
             scores = jnp.where(same, scores, MASKED)
             top = jnp.max(scores, axis=-1, keepdims=True)
@@ -103,6 +121,11 @@
             part = dot_nn(probs, jnp.where(mine, v, zero))
             out = part if out is None else out + part
         o_ref[tile : tile + TILE, :] = out.astype(bf16)
+
+    @pl.when(step == last)
+    def _():
+        outof.wait()
+        wait_all(blocks)
 
 
 def middle_kernel(
@@ -160,10 +183,77 @@
     do_ref[...] = dot_nt(low, w_out_ref[...]).astype(bf16)
 
 
-def attend_back_kernel(
-    q_ref, k_ref, v_ref, o_ref, do_ref, p_ref, cos_ref, sin_ref,
-    dq_ref, dk_ref, dv_ref, key_sum, value_sum,
-):
+def early_order(sizes, rep_first):
+    fsdp, rep, _ = sizes
+    core = [("fsdp", 1)]
+    rest = [("fsdp", b) for b in bits_of(fsdp)[1:]]
+    copies = [("rep", b) for b in bits_of(rep)]
+    return core + (copies + rest if rep_first else rest + copies)
+
+
+def late_order(sizes):
+    return [("seq", b) for b in bits_of(sizes[2])]
+
+
+def early_reducers(sizes, shapes):
+    orders = [early_order(sizes, w == 2) for w in range(3)]
+    early = len(orders[0])
+    return [Reducer(shape, sizes, order + late_order(sizes)) for shape, order in zip(shapes, orders)], early
+
+
+def attend_back_kernel(sizes, shapes, q_ref, k_ref, v_ref, o_ref, do_ref, p_ref, cos_ref, sin_ref, y_ref, *refs):
+    count = len(shapes)
+    reducers, early = early_reducers(sizes, shapes)
+    refs = list(refs)
+    pop = lambda n: [refs.pop(0) for _ in range(n)]
+    grads = pop(count)
+    dq_ref, dk_ref, dv_ref, home_ref = pop(4)
+    sums_out = pop(count)
+    key_sum, value_sum, bounce = pop(3)
+    kept = pop(count)
+    lands = [pop(len(r.scratch(0, early))) for r in reducers]
+    sems = Sems(*refs)
+    me = lax.axis_index("fsdp")
+    step, last = pl.program_id(0), pl.num_programs(0) - 1
+    into, outof, blocks = give_back(y_ref, home_ref, bounce, sems)
+    loads, stores = [], []
+    for w, reducer in enumerate(reducers):
+        keep = reducer.steps[0]["keep"]
+        for j in keep:
+            loads.append(sems.copy(grads[w].at[flip(me, j)], kept[w].at[j // 2]))
+        stores.append(sems.copy(kept[w].at[0], sums_out[w]))
+        parts = lambda j, w=w: kept[w].at[j // 2] if j % 2 == 0 else grads[w].at[flip(me, j)]
+        reducer.bind(parts, lands[w], sems, 0, early)
+
+    @pl.when(step == 0)
+    def _():
+        into.start()
+        start_all(loads)
+        meet(
+            [("seq", k) for k in range(1, sizes[2])]
+            + [("fsdp", b) for b in bits_of(sizes[0])]
+            + [("rep", b) for b in bits_of(sizes[1])]
+        )
+        for reducer in reducers:
+            reducer.start(0)
+        start_all(blocks)
+        into.wait()
+        outof.start()
+
+    @pl.when(step == 1)
+    def _():
+        wait_all(loads)
+        for reducer in reducers:
+            reducer.finish(0)
+            reducer.start(1)
+
+    for w, reducer in enumerate(reducers):
+        for s in range(1, early - 1):
+            @pl.when(step == min(2 + w + s, 5))
+            def _(reducer=reducer, s=s):
+                reducer.finish(s)
+                reducer.start(s + 1)
+
     k, v = k_ref[...], v_ref[...]
     lane = lax.broadcasted_iota(jnp.int32, (1, PAIR), 1)
     length = k.shape[0]
@@ -196,6 +286,86 @@
     dk_ref[...] = rotate_pair(key_sum[...], cosine, -sine).astype(bf16)
     dv_ref[...] = value_sum[...].astype(bf16)
 
+    @pl.when(step == last)
+    def _():
+        for w, reducer in enumerate(reducers):
+            reducer.finish(early - 1)
+            stores[w].start()
+        wait_all(stores)
+        outof.wait()
+        wait_all(blocks)
+
+
+def leave_kernel(sizes, shapes, late_shapes, dx_ref, gains_ref, *refs):
+    count, more = len(shapes), len(late_shapes)
+    fsdp, rep, seq = sizes
+    reducers, early = early_reducers(sizes, shapes)
+    whole = [Reducer(shape, sizes, early_order(sizes, w == 1) + late_order(sizes)) for w, shape in enumerate(late_shapes)]
+    refs = list(refs)
+    pop = lambda n: [refs.pop(0) for _ in range(n)]
+    sums_in, grads = pop(count), pop(more)
+    (home_ref,) = pop(1)
+    sums_out, wholes_out = pop(count), pop(more)
+    (gains_out,) = pop(1)
+    (bounce,) = pop(1)
+    held, kept, finals = pop(count), pop(more), pop(count + more)
+    lands = [pop(len(r.scratch(early, len(r.steps)))) for r in reducers]
+    whole_lands = [pop(len(r.scratch(0, len(r.steps)))) for r in whole]
+    (gain_lands,) = pop(1)
+    sems = Sems(*refs)
+    me = lax.axis_index("fsdp")
+    into, outof, blocks = give_back(dx_ref, home_ref, bounce, sems)
+    loads = [sems.copy(sums_in[w], held[w]) for w in range(count)]
+    stores = [sems.copy(finals[w], out) for w, out in enumerate(sums_out + wholes_out)]
+    for w, reducer in enumerate(reducers):
+        reducer.bind(lambda j, w=w: held[w], lands[w], sems, early, len(reducer.steps), finals[w])
+    whole_loads = []
+    for w, reducer in enumerate(whole):
+        whole_loads.append([sems.copy(grads[w].at[flip(me, j)], kept[w].at[j // 2]) for j in reducer.steps[0]["keep"]])
+        parts = lambda j, w=w: kept[w].at[j // 2] if j % 2 == 0 else grads[w].at[flip(me, j)]
+        reducer.bind(parts, whole_lands[w], sems, 0, len(reducer.steps), finals[count + w])
+    partners = [("seq", k) for k in range(1, seq)] + [("fsdp", b) for b in bits_of(fsdp)] + [("rep", b) for b in bits_of(rep)]
+    hops = [("fsdp", b) for b in bits_of(fsdp)] + [("rep", b) for b in bits_of(rep)] + [("seq", b) for b in bits_of(seq)]
+    gain_moves = [sems.remote(gains_out, gain_lands.at[i], axis, bit) for i, (axis, bit) in enumerate(hops)]
+    into.start()
+    start_all(loads)
+    for group in whole_loads:
+        start_all(group)
+    gains_out[...] = gains_ref[...]
+    meet(partners)
+    for reducer in whole:
+        reducer.start(0)
+    gain_moves[0].start()
+    start_all(blocks)
+    wait_all(loads)
+    for reducer in reducers:
+        reducer.start(early)
+    into.wait()
+    outof.start()
+    for group in whole_loads:
+        wait_all(group)
+    longest = max(len(r.steps) for r in whole)
+    for s in range(longest):
+        for reducer in whole:
+            if s < len(reducer.steps):
+                reducer.finish(s)
+                if s + 1 < len(reducer.steps):
+                    reducer.start(s + 1)
+        for reducer in reducers:
+            if s + early < len(reducer.steps):
+                reducer.finish(s + early)
+                if s + early + 1 < len(reducer.steps):
+                    reducer.start(s + early + 1)
+        if s < len(hops):
+            gain_moves[s].wait()
+            gains_out[...] += gain_lands[s]
+            if s + 1 < len(hops):
+                gain_moves[s + 1].start()
+    start_all(stores)
+    wait_all(stores)
+    outof.wait()
+    wait_all(blocks)
+
 
 def last_kernel(dq_ref, dk_ref, dv_ref, x_ref, dx1_ref, gain_ref, w_ref, dx_ref, dgain_ref):
     da = dot_nt(dq_ref[...], w_ref[:, :D])
@@ -228,7 +398,7 @@
     return jax.ShapeDtypeStruct(shape, dtype)
 
 
-def call(kernel, grid, in_specs, out_specs, out_shape, flops, scratch=()):
+def call(kernel, grid, in_specs, out_specs, out_shape, flops, scratch=(), collective=None):
     return pl.pallas_call(
         kernel,
         grid=(grid,),
@@ -237,87 +407,274 @@
         out_shape=out_shape,
         scratch_shapes=list(scratch),
         compiler_params=pltpu.CompilerParams(
-            dimension_semantics=("arbitrary",), vmem_limit_bytes=VMEM_LIMIT
+            dimension_semantics=("arbitrary",), vmem_limit_bytes=VMEM_LIMIT,
+            collective_id=collective, has_side_effects=collective is not None,
         ),
         cost_estimate=pl.CostEstimate(flops=flops, bytes_accessed=10 * 2**20, transcendentals=0),
     )
 
 
-def exchange(array, axis, mask, size):
-    return lax.ppermute(array, axis, [(i, i ^ mask) for i in range(size)])
+MESH = pl.DeviceIdType.MESH
+ANY = pl.BlockSpec(memory_space=pl.ANY)
 
 
 def take(array, index):
     return lax.dynamic_index_in_dim(array, index, 0, keepdims=False)
 
 
-def swap_blocks(blocks, me, size):
-    received = [take(blocks, me)]
-    for k in range(1, size):
-        received.append(exchange(take(blocks, me ^ k), "seq", k, size))
-    return received
-
-
-def swap_back(slots, me, size):
-    arrived = jnp.stack(
-        [slots[0]] + [exchange(slots[k], "seq", k, size) for k in range(1, size)]
+def flip(index, mask):
+    bit = 1
+    while bit <= mask:
+        if mask & bit:
+            index = index + bit - 2 * bit * ((index // bit) % 2)
+        bit *= 2
+    return index
+
+
+def bits_of(size):
+    return [1 << i for i in range(size.bit_length() - 1)]
+
+
+def meet(partners):
+    barrier = pltpu.get_barrier_semaphore()
+    for axis, mask in partners:
+        pl.semaphore_signal(
+            barrier, inc=1, device_id={axis: flip(lax.axis_index(axis), mask)}, device_id_type=MESH
+        )
+    pl.semaphore_wait(barrier, len(partners))
+
+
+class Sems:
+    def __init__(self, send, recv, local):
+        self.send, self.recv, self.local = send, recv, local
+        self.remote_used = self.local_used = 0
+
+    def remote(self, src, dst, axis, mask):
+        i = self.remote_used
+        self.remote_used += 1
+        return pltpu.make_async_remote_copy(
+            src_ref=src, dst_ref=dst, send_sem=self.send.at[i], recv_sem=self.recv.at[i],
+            device_id={axis: flip(lax.axis_index(axis), mask)}, device_id_type=MESH,
+        )
+
+    def copy(self, src, dst):
+        i = self.local_used
+        self.local_used += 1
+        return pltpu.make_async_copy(src, dst, self.local.at[i])
+
+
+def sem_shapes(remote, local):
+    dma = pltpu.SemaphoreType.DMA
+    return [dma((remote,)), dma((remote,)), dma((max(local, 1),))]
+
+
+def start_all(copies):
+    for copy in copies:
+        copy.start()
+
+
+def wait_all(copies):
+    for copy in copies:
+        copy.wait()
+
+
+def enter_kernel(sizes, count, *refs):
+    fsdp, rep, seq = sizes
+    tokens, shards = refs[0], refs[1 : 1 + count]
+    x_out, fulls = refs[1 + count], refs[2 + count : 2 + 2 * count]
+    bounce_x, bounces = refs[2 + 2 * count], refs[3 + 2 * count : 3 + 3 * count]
+    sems = Sems(*refs[3 + 3 * count :])
+    me, me_seq, me_rep = lax.axis_index("fsdp"), lax.axis_index("seq"), lax.axis_index("rep")
+    into = [sems.copy(tokens.at[me_seq], bounce_x)] + [sems.copy(shards[w], bounces[w]) for w in range(count)]
+    outof = [sems.copy(bounce_x, x_out.at[0])] + [sems.copy(bounces[w], fulls[w].at[me]) for w in range(count)]
+    start_all(into)
+    meet([("seq", k) for k in range(1, seq)] + [("fsdp", b) for b in bits_of(fsdp)] + [("rep", b) for b in bits_of(rep)])
+    blocks = [sems.remote(tokens.at[flip(me_seq, k)], x_out.at[k], "seq", k) for k in range(1, seq)]
+    start_all(blocks)
+
+    def piece(ref, w, index):
+        width = shards[w].shape[-1] // rep
+        return ref.at[index, :, pl.ds(pl.multiple_of(me_rep * width, 128), width)]
+
+    def first_piece(w):
+        width = shards[w].shape[-1] // rep
+        return shards[w].at[:, pl.ds(pl.multiple_of(me_rep * width, 128), width)]
+
+    held = [0]
+    pending = []
+    for bit in reversed(bits_of(fsdp)[1:]):
+        over = []
+        for w in range(count):
+            moved = []
+            for h in held:
+                src = first_piece(w) if h == 0 else piece(fulls[w], w, flip(me, h))
+                moved.append(sems.remote(src, piece(fulls[w], w, flip(me, h)), "fsdp", bit))
+            start_all(moved)
+            over.append(moved)
+        relays = []
+        for w in range(count):
+            for copy in over[w]:
+                copy.wait_recv()
+            moved = []
+            for mask in range(1, rep):
+                for h in held:
+                    here = piece(fulls[w], w, flip(me, h ^ bit))
+                    moved.append(sems.remote(here, here, "rep", mask))
+            start_all(moved)
+            relays.append(moved)
+            pending += over[w]
+        for moved in relays:
+            for copy in moved:
+                copy.wait_recv()
+            pending += moved
+        held = held + [h ^ bit for h in held]
+    last = []
+    for w in range(count):
+        for h in held:
+            src = shards[w] if h == 0 else fulls[w].at[flip(me, h)]
+            last.append(sems.remote(src, fulls[w].at[flip(me, h)], "fsdp", 1))
+    start_all(last)
+    wait_all(into)
+    start_all(outof)
+    for copy in pending:
+        copy.wait_send()
+    wait_all(last)
+    wait_all(blocks)
+    wait_all(outof)
+
+
+def enter(sizes, tokens, shards):
+    fsdp, rep, seq = sizes
+    count = len(shards)
+    assert fsdp >= 2
+    held, copies = 1, seq - 1
+    for _ in bits_of(fsdp)[1:]:
+        copies += count * held * rep
+        held *= 2
+    copies += count * held
+    hbm = lambda shape: struct(bf16, *shape)
+    return pl.pallas_call(
+        functools.partial(enter_kernel, sizes, count),
+        in_specs=[ANY] * (1 + count),
+        out_specs=[ANY] * (1 + count),
+        out_shape=[hbm(tokens.shape)] + [hbm((fsdp,) + s.shape) for s in shards],
+        scratch_shapes=[pltpu.VMEM(tokens.shape[1:], bf16)]
+        + [pltpu.VMEM(s.shape, bf16) for s in shards]
+        + sem_shapes(copies, 2 * (1 + count)),
+        compiler_params=pltpu.CompilerParams(collective_id=0, has_side_effects=True),
+    )(tokens, *shards)
+
+
+class Reducer:
+    def __init__(self, parts_shape, sizes, order):
+        self.fsdp, self.rows, self.cols = parts_shape
+        self.steps = []
+        held, rows, cols = list(range(self.fsdp)), self.rows, self.cols
+        row_at, col_at = [], []
+        for axis, bit in order:
+            step = dict(axis=axis, bit=bit, row_at=list(row_at), col_at=list(col_at), rows=rows, cols=cols)
+            if axis == "fsdp":
+                step["send"] = [j for j in held if j & bit]
+                held = [j for j in held if not j & bit]
+                step["keep"] = held
+                step["shape"] = (len(held), rows, cols)
+                step["split"] = None
+            else:
+                step["keep"] = step["send"] = held
+                if (rows // 2) % 16 == 0:
+                    rows //= 2
+                    row_at = row_at + [(axis, bit, rows)]
+                    step["split"] = "rows"
+                elif (cols // 2) % 128 == 0:
+                    cols //= 2
+                    col_at = col_at + [(axis, bit, cols)]
+                    step["split"] = "cols"
+                else:
+                    step["split"] = "none"
+                step["shape"] = (len(held), rows, cols)
+            self.steps.append(step)
+        self.down = len(self.steps)
+        for step in reversed(self.steps[: self.down]):
+            if step["split"] in ("rows", "cols"):
+                self.steps.append(dict(step, up=True))
+
+    @staticmethod
+    def offset(terms, align, last=None):
+        total = 0
+        for i, (axis, bit, extent) in enumerate(terms):
+            half = (lax.axis_index(axis) // bit) % 2
+            if last == i:
+                half = 1 - half
+            total = total + half * extent
+        return total if isinstance(total, int) else pl.multiple_of(total, align)
+
+    def region(self, step, after, other=False):
+        row_at, col_at, rows, cols = step["row_at"], step["col_at"], step["rows"], step["cols"]
+        row_last = col_last = None
+        if after:
+            if step["split"] == "rows":
+                rows //= 2
+                row_at = row_at + [(step["axis"], step["bit"], rows)]
+                row_last = len(row_at) - 1 if other else None
+            elif step["split"] == "cols":
+                cols //= 2
+                col_at = col_at + [(step["axis"], step["bit"], cols)]
+                col_last = len(col_at) - 1 if other else None
+        return (
+            pl.ds(self.offset(row_at, 16, row_last), rows),
+            pl.ds(self.offset(col_at, 128, col_last), cols),
+        )
+
+    def scratch(self, first, last):
+        return [pltpu.VMEM(s["shape"], bf16) for s in self.steps[first:last] if "up" not in s]
+
+    def copies(self, first, last):
+        return sum(1 if "up" in s else len(s["send"]) for s in self.steps[first:last])
+
+    def bind(self, parts, lands, sems, first, last, final=None):
+        self.parts, self.sems, self.final = parts, sems, final
+        self.lands, self.moves = {}, {}
+        lands = list(lands)
+        for s in range(first, last):
+            step = self.steps[s]
+            moves = []
+            if "up" in step:
+                there = final.at[self.region(step, True)]
+                moves.append(sems.remote(there, there, step["axis"], step["bit"]))
+            else:
+                land = self.lands[s] = lands.pop(0)
+                for i, j in enumerate(step["send"]):
+                    fsdp = step["axis"] == "fsdp"
+                    src = self.parts(j).at[self.region(step, not fsdp, not fsdp)]
+                    moves.append(sems.remote(src, land.at[i], step["axis"], step["bit"]))
+            self.moves[s] = moves
+
+    def start(self, s):
+        start_all(self.moves[s])
+
+    def finish(self, s):
+        step = self.steps[s]
+        for i, move in enumerate(self.moves[s]):
+            move.wait()
+            if "up" not in step:
+                j = step["keep"][i]
+                ref = self.parts(j)
+                region = self.region(step, True)
+                total = (ref[region].astype(f32) + self.lands[s][i].astype(f32)).astype(bf16)
+                if s == self.down - 1:
+                    self.final[region] = total
+                else:
+                    ref[region] = total
+
+
+def give_back(slots, home, bounce, sems):
+    me = lax.axis_index("seq")
+    seq = slots.shape[0]
+    return (
+        sems.copy(slots.at[0], bounce),
+        sems.copy(bounce, home.at[me]),
+        [sems.remote(slots.at[k], home.at[me], "seq", k) for k in range(1, seq)],
     )
-    return jnp.stack([take(arrived, me ^ s) for s in range(size)])
-
-
-def gather_weight(shard, me, size):
-    parts = shard[None]
-    bit = size // 2
-    while bit:
-        parts = jnp.concatenate([parts, exchange(parts, "fsdp", bit, size)], 0)
-        bit //= 2
-    order = [0]
-    bit = size // 2
-    while bit:
-        order = order + [o ^ bit for o in order]
-        bit //= 2
-    back = [order.index(j) for j in range(size)]
-    relative = [parts[back[j]] for j in range(size)]
-    stacked = jnp.stack(relative)
-    ordered = jnp.stack([take(stacked, me ^ j) for j in range(size)])
-    return ordered.reshape((size * shard.shape[0],) + shard.shape[1:])
-
-
-def add_low(left, right):
-    return (left.astype(f32) + right.astype(f32)).astype(bf16)
-
-
-def reduce_packed(packed, sizes):
-    fsdp, rep, seq = sizes
-    me = lax.axis_index("fsdp")
-    array = jnp.stack([take(packed, me ^ j) for j in range(fsdp)])
-    bit = 1
-    while bit < fsdp:
-        halves = array.reshape((array.shape[0] // 2, 2) + array.shape[1:])
-        array = add_low(halves[:, 0], exchange(halves[:, 1], "fsdp", bit, fsdp))
-        bit *= 2
-    array = array[0]
-    steps = []
-    for axis, size in (("rep", rep), ("seq", seq)):
-        bit = 1
-        while bit < size:
-            steps.append((axis, bit, size))
-            bit *= 2
-    for axis, bit, size in steps:
-        mine = (lax.axis_index(axis) // bit) % 2
-        halves = array.reshape(2, array.shape[0] // 2, array.shape[1])
-        array = add_low(take(halves, mine), exchange(take(halves, 1 - mine), axis, bit, size))
-    for axis, bit, size in reversed(steps):
-        mine = (lax.axis_index(axis) // bit) % 2
-        other = exchange(array, axis, bit, size)
-        first = jnp.where(mine == 0, array, other)
-        second = jnp.where(mine == 0, other, array)
-        array = jnp.concatenate([first, second], 0)
-    return array
-
-
-def padded_rows(rows, align):
-    return -(-rows // align) * align
 
 
 def body(sizes, tokens, segments, positions, gain_attn, w_qkv, w_out, gain_mlp, w_in, w_mlp_out, cotangent):
@@ -327,8 +684,15 @@
     length = seq * rows
     me_seq, me_fsdp = lax.axis_index("seq"), lax.axis_index("fsdp")
 
-    x_slots = swap_blocks(tokens.reshape(seq, rows, D), me_seq, seq)
-    x = jnp.concatenate(x_slots, 0)
+    own_gains = jnp.zeros((16, D), bf16)
+    own_gains = lax.dynamic_update_slice(own_gains, jnp.stack([gain_attn, gain_mlp]), (0, me_fsdp * (D // fsdp)))
+    x, gains, wq, wo, wm, wi = enter(
+        sizes, tokens.reshape(seq, rows, D), [own_gains, w_qkv, w_out, w_mlp_out, w_in]
+    )
+    x = x.reshape(length, D)
+    gains = jnp.sum(gains[:, :2].astype(f32), axis=0)
+    gain_one, gain_two = gains[:1], gains[1:]
+    wq, wo, wm, wi = (w.reshape(-1, w.shape[-1]) for w in (wq, wo, wm, wi))
 
     marks = take(segments.reshape(seq, length), me_seq)
     place = jnp.arange(length, dtype=jnp.int32) - jnp.sum(
@@ -343,11 +707,6 @@
     cosine = jnp.concatenate([cosine] * 4, -1)
     sine = jnp.concatenate([-sine, sine] * 2, -1)
 
-    gather = lambda shard: gather_weight(shard, me_fsdp, fsdp)
-    gains = gather(jnp.stack([gain_attn, gain_mlp], 1)).astype(f32)
-    gain_one, gain_two = gains[:, 0][None], gains[:, 1][None]
-    wq = gather(w_qkv)
-
     tiles, pairs = length // TILE, HEADS // 2
     a, qkv = call(
         first_kernel, tiles,
@@ -358,16 +717,17 @@
     )(x, gain_one, wq, cosine, sine)
 
     prob_spec = pl.BlockSpec((2, length, length), lambda i: (i, 0, 0))
-    o, probs = call(
-        attend_kernel, pairs,
+    o, probs, dy = call(
+        functools.partial(attend_kernel, sizes), pairs,
         [pair_spec(length), pair_spec(length, pairs), pair_spec(length, 2 * pairs),
-         whole_spec(length, 1), whole_spec(1, length)],
-        [pair_spec(length), prob_spec],
-        [struct(bf16, length, D), struct(bf16, HEADS, length, length)],
+         whole_spec(length, 1), whole_spec(1, length), ANY],
+        [pair_spec(length), prob_spec, ANY],
+        [struct(bf16, length, D), struct(bf16, HEADS, length, length), struct(bf16, seq, rows, D)],
         16 * length * length * D,
-    )(qkv, qkv, qkv, marks[:, None], marks[None, :])
-
-    wo, wi, wm = gather(w_out), gather(w_in), gather(w_mlp_out)
+        [pltpu.VMEM((rows, D), bf16)] + sem_shapes(seq - 1, 2), 1,
+    )(qkv, qkv, qkv, marks[:, None], marks[None, :], cotangent.reshape(seq, rows, D))
+    dy = dy.reshape(length, D)
+
     x1, b, m, slope, act, y = call(
         middle_kernel, tiles,
         [rows_spec(D), rows_spec(D), whole_spec(1, D), whole_spec(D, D), whole_spec(D, 2 * FF), whole_spec(FF, D)],
@@ -376,9 +736,6 @@
          struct(bf16, length, FF), struct(bf16, length, FF), struct(bf16, length, D)],
         2 * length * (D * D + 3 * D * FF),
     )(o, x, gain_two, wo, wi, wm)
-    block_out = swap_back([y[k * rows : (k + 1) * rows] for k in range(seq)], me_seq, seq)
-
-    dy = jnp.concatenate(swap_blocks(cotangent.reshape(seq, rows, D), me_seq, seq), 0)
     dh, low, dx1, do, dgain_two = call(
         middle_back_kernel, tiles,
         [rows_spec(D), rows_spec(D), rows_spec(FF), rows_spec(FF), whole_spec(1, D),
@@ -389,26 +746,25 @@
         2 * length * (D * D + 3 * D * FF),
     )(dy, x1, slope, act, gain_two, wo, wi, wm)
 
-    grad_mlp = dot_tn(m, dy).astype(bf16).reshape(fsdp, FF // fsdp, D)
-    grad_in = dot_tn(b, dh).astype(bf16).reshape(fsdp, D // fsdp, 3, D).swapaxes(1, 2).reshape(fsdp, 3 * D // fsdp, D)
-    grad_out = dot_tn(o, low).astype(bf16).reshape(fsdp, D // fsdp, D)
-    parts = [grad_out, grad_mlp, grad_in]
-    used = sum(part.shape[1] for part in parts)
-    align = 8 * rep * seq
-    spare = padded_rows(used, align) - used
-    if spare:
-        parts.append(jnp.zeros((fsdp, spare, D), bf16))
-    reduced = reduce_packed(jnp.concatenate(parts, 1), sizes)
-
-    dq, dk, dv = call(
-        attend_back_kernel, pairs,
+    grads = [dot_tn(m, dy), dot_tn(o, low), dot_tn(b, dh)]
+    grads = [g.astype(bf16).reshape(fsdp, g.shape[0] // fsdp, g.shape[1]) for g in grads]
+    shapes = [g.shape for g in grads]
+    reducers, early = early_reducers(sizes, shapes)
+    halves = fsdp // 2
+    quarter = lambda shape: struct(bf16, *shape[1:])
+    dq, dk, dv, block_out, *sums = call(
+        functools.partial(attend_back_kernel, sizes, shapes), pairs,
         [pair_spec(length), pair_spec(length, pairs), pair_spec(length, 2 * pairs),
-         pair_spec(length), pair_spec(length), prob_spec, whole_spec(length, PAIR), whole_spec(length, PAIR)],
-        [pair_spec(length)] * 3,
-        [struct(bf16, length, D)] * 3,
+         pair_spec(length), pair_spec(length), prob_spec, whole_spec(length, PAIR), whole_spec(length, PAIR)]
+        + [ANY] * 4,
+        [pair_spec(length)] * 3 + [ANY] * 4,
+        [struct(bf16, length, D)] * 3 + [struct(bf16, seq, rows, D)] + [quarter(s) for s in shapes],
         32 * length * length * D,
-        [pltpu.VMEM((length, PAIR), f32)] * 2,
-    )(qkv, qkv, qkv, o, do, probs, cosine, sine)
+        [pltpu.VMEM((length, PAIR), f32)] * 2 + [pltpu.VMEM((rows, D), bf16)]
+        + [pltpu.VMEM((halves,) + s[1:], bf16) for s in shapes]
+        + [land for r in reducers for land in r.scratch(0, early)]
+        + sem_shapes(seq - 1 + sum(r.copies(0, early) for r in reducers), 2 + 3 * (halves + 1)), 2,
+    )(qkv, qkv, qkv, o, do, probs, cosine, sine, y.reshape(seq, rows, D), *grads)
 
     dx, dgain_one = call(
         last_kernel, tiles,
@@ -417,35 +773,44 @@
         [struct(bf16, length, D), struct(f32, 1, D)],
         2 * length * D * 3 * D,
     )(dq, dk, dv, x, dx1, gain_one, wq)
-    input_grad = swap_back([dx[k * rows : (k + 1) * rows] for k in range(seq)], me_seq, seq)
-
-    grad_qkv = dot_tn(a, jnp.concatenate([dq, dk, dv], 1)).astype(bf16).reshape(fsdp, D // fsdp, 3 * D)
-    spare = padded_rows(D // fsdp, align) - D // fsdp
-    if spare:
-        grad_qkv = jnp.pad(grad_qkv, ((0, 0), (0, spare), (0, 0)))
-    qkv_reduced = reduce_packed(grad_qkv, sizes)[: D // fsdp].astype(f32)
-
-    dgains = jnp.concatenate([dgain_one, dgain_two], 0)
-    for axis, size in (("fsdp", fsdp), ("rep", rep), ("seq", seq)):
-        bit = 1
-        while bit < size:
-            dgains = dgains + exchange(dgains, axis, bit, size)
-            bit *= 2
+    late = [dot_tn(a, part).astype(bf16).reshape(fsdp, D // fsdp, D) for part in (dq, dk, dv)]
+    late_shapes = [g.shape for g in late]
+    whole = [Reducer(s, sizes, early_order(sizes, w == 1) + late_order(sizes)) for w, s in enumerate(late_shapes)]
+    dgains = jnp.concatenate([dgain_one, dgain_two, jnp.zeros((6, D), f32)], 0)
+    hops = sum(len(bits_of(n)) for n in sizes)
+    vmem = pl.BlockSpec(memory_space=pltpu.VMEM)
+    input_grad, *results, dgains = pl.pallas_call(
+        functools.partial(leave_kernel, sizes, shapes, late_shapes),
+        in_specs=[ANY, vmem] + [ANY] * 6,
+        out_specs=[ANY] * 7 + [vmem],
+        out_shape=[struct(bf16, seq, rows, D)] + [quarter(s) for s in shapes + late_shapes] + [struct(f32, 8, D)],
+        scratch_shapes=[pltpu.VMEM((rows, D), bf16)]
+        + [pltpu.VMEM(s[1:], bf16) for s in shapes]
+        + [pltpu.VMEM((halves,) + s[1:], bf16) for s in late_shapes]
+        + [pltpu.VMEM(s[1:], bf16) for s in shapes + late_shapes]
+        + [land for r in reducers for land in r.scratch(early, len(r.steps))]
+        + [land for r in whole for land in r.scratch(0, len(r.steps))]
+        + [pltpu.VMEM((hops, 8, D), f32)]
+        + sem_shapes(
+            seq - 1 + hops + sum(r.copies(early, len(r.steps)) for r in reducers)
+            + sum(r.copies(0, len(r.steps)) for r in whole),
+            2 + 2 * len(shapes) + len(late_shapes) * (halves + 1),
+        ),
+        compiler_params=pltpu.CompilerParams(
+            collective_id=3, has_side_effects=True, vmem_limit_bytes=VMEM_LIMIT
+        ),
+    )(dx.reshape(seq, rows, D), dgains, *sums, *late)
     dgains = lax.dynamic_slice_in_dim(dgains, me_fsdp * (D // fsdp), D // fsdp, 1)
-
-    first = D // fsdp
-    second = first + FF // fsdp
-    third = second + 3 * D // fsdp
-    full = reduced.astype(f32)
+    grad_mlp, grad_out, grad_in, grad_q, grad_k, grad_v = (r.astype(f32) for r in results)
     return (
         block_out.reshape(tokens.shape),
         input_grad.astype(f32).reshape(tokens.shape),
         dgains[0],
-        qkv_reduced,
-        full[:first],
+        jnp.concatenate([grad_q, grad_k, grad_v], 1),
+        grad_out,
         dgains[1],
-        full[second:third].reshape(3, D // fsdp, D).swapaxes(0, 1).reshape(D // fsdp, 3 * D),
-        full[first:second],
+        grad_in,
+        grad_mlp,
     )
 
 

time: 420 us -> 337 us (0.80)
  Pallas kernels: 123 us -> 288 us
  waiting for transfers between devices: 149 us -> 0 us
  starting transfers between devices: 49.5 us -> 0 us
  local copies, waits for them, and re-layouts: 33.7 us -> 7.67 us
  other arithmetic: 38.9 us -> 14.9 us
  matrix products: 17.4 us -> 22.5 us
    pallas_call x2 -> x4, Pallas kernels: 68.5 us -> 233 us  [the longest x1 90.7 us: body(): pl.pallas_call(functools.partial(leave_kernel, sizes, shapes, late_shapes...]
    ppermute x43 -> x0, waiting for transfers between devices: 149 us -> none  [exchange(): return lax.ppermute(array, axis, [(i, i ^ mask) for i in range(size)])]
    ppermute x43 -> x0, starting transfers between devices: 49.5 us -> none  [exchange(): return lax.ppermute(array, axis, [(i, i ^ mask) for i in range(size)])]
    another operation x15 -> x1, other arithmetic: 13.5 us -> 0.01 us  [body(): jnp.stack([gain_attn, gain_mlp])]
    reshape x2 -> x0, local copies, waits for them, and re-layouts: 9.95 us -> none  [the longest x1 8.73 us: body(): dot_tn(b, dh).astype(bf16).reshape(fsdp, D // fsdp, 3, D).swapaxes(1, 2)]
    squeeze x12 -> x0, local copies, waits for them, and re-layouts: 5.59 us -> none  [the longest x8 3.88 us: take(): return lax.dynamic_index_in_dim(array, index, 0, keepdims=False)]
    concatenate x13 -> x2, other arithmetic: 9.28 us -> 3.94 us  [the longest x1 2.58 us: body(): jnp.concatenate([grad_q, grad_k, grad_v], 1)]
    dot_general x4 -> x6, matrix products: 17.4 us -> 22.5 us  [dot_tn(): lax.dot_general(left, right, (((0,), (0,)), ((), ())), preferred_element_...]
  transfers between devices with their start and end apart: 43 -> 0, of which waited for: 21 -> 0; matrix products, arithmetic and copies ran while one was open for 17% -> 0% of each run, Pallas kernels for 15% -> 0%
where the time goes in v2:
time: 337 us; the launch traced here: 334 us
  Pallas kernels  288 us (85%)
  matrix products  22.5 us (7%)
  other arithmetic  14.9 us (4%)
  local copies, waits for them, and re-layouts  7.67 us (2%)
    pallas_call x1, Pallas kernels, body(): pl.pallas_call(functools.partial(leave_kernel, sizes, shapes, late_shapes...  90.7 us
    pallas_call x1, Pallas kernels, enter(): pl.pallas_call(functools.partial(enter_kernel, sizes, count), in_specs=[A...  54.9 us
    pallas_call x1, Pallas kernels, body(): call(functools.partial(attend_back_kernel, sizes, shapes), pairs, [pair_s...  51.7 us
    pallas_call x1, Pallas kernels, body(): call(functools.partial(attend_kernel, sizes), pairs, [pair_spec(length),...  35.3 us
    dot_general x6, matrix products, dot_tn(): lax.dot_general(left, right, (((0,), (0,)), ((), ())), preferred_element_...  22.5 us
    pallas_call x1, Pallas kernels, body(): call(middle_back_kernel, tiles, [rows_spec(D), rows_spec(D), rows_spec(FF...  18.3 us
    pallas_call x1, Pallas kernels, body(): call(middle_kernel, tiles, [rows_spec(D), rows_spec(D), whole_spec(1, D),...  17.3 us
    pallas_call x1, Pallas kernels, body(): call(last_kernel, tiles, [rows_spec(D)] * 5 + [whole_spec(1, D), whole_sp...  10.2 us

profile of v2, /device:TPU:0, one launch (start us, length us, event | category | flops | bytes accessed | tf_op | source)
XLA Modules:
  0.0 333.7 jit_solution(16202112794186122375)
XLA Ops:
  3.2 1.9 fusion
  5.2 1.3 pad_maximum_fusion.1.sin_ref
  6.4 1.3 pad_maximum_fusion.cos_ref
  9.1 54.9 %shard_map.152 = (bf16[4,256,768]{2,1,0:T(8,128)(2,1)}, bf16[4,16,768]{2,1,0:T(8,128)(2,1)}, bf16[4,192,2304]{2,1,0:T(8,128)(2,1)}, bf16[4,192,768]{2,1,0:T(8,12...) custom-call(bf16[4,256,768]{2,1,0:T(8,128)(2,1)} %bitcast.45, bf16[16,768]{1,0:T(8,128)(2,1)} %copy-done.5, ...), custom_call_target="tpu_custom_call" | custom-call | tf_op jit(solution)/shard_map/pallas_call | solution.py:556
  65.5 9.2 %shard_map.153 = (bf16[1024,768]{1,0:T(8,128)(2,1)}, bf16[1024,2304]{1,0:T(8,128)(2,1)}) custom-call(bf16[1024,768]{1,0:T(8,128)(2,1)} %bitcast.71, f32[1,768]{1,0:T(1,128)} %get-tuple-element.91.gain_ref, bf16[768,2304]{1,0:T(8,128)(2,1)} %bitcast.64, f32[1024,128]{1,0:T(8,128)} %pad_maximum_fusion.cos_ref, f32[1024,128]{1,0:T(8,128)} %pad_maximum_fusion.1.sin_ref), custom_call_target="tpu_custom_call" | custom-call | flops 3623878656 | bytes 10485760 | tf_op jit(solution)/shard_map/pallas_call | solution.py:711
  74.7 1.0 copy.20.rows_ref
  75.7 35.3 %shard_map.154 = (bf16[1024,768]{1,0:T(8,128)(2,1)}, bf16[12,1024,1024]{2,1,0:T(8,128)(2,1)}, bf16[4,256,768]{2,1,0:T(8,128)(2,1)}) custom-call(bf16[1024,2304]{1,0:T(8,128)(2,1)} %get-tuple-element.50.q_ref.k_ref.v_ref, bf16[1024,2304]{1,0:T(8,128)(2,1)} %get-tuple-element.50.q_ref.k_ref.v_ref, bf16[1024,2304]{1,0:T(8,128)(2,1)} %get-tuple-element.50.q_ref.k_ref.v_ref, ...), custom_call_target="tpu_custom_call" | custom-call | flops 12884901888 | bytes 10485760 | tf_op jit(solution)/shard_map/pallas_call | solution.py:720
  111.0 17.3 %shard_map.155 = (f32[1024,768]{1,0:T(8,128)}, bf16[1024,768]{1,0:T(8,128)(2,1)}, bf16[1024,1152]{1,0:T(8,128)(2,1)}, bf16[1024,1152]{1,0:T(8,128)(2,1)}, bf16[1...) custom-call(bf16[1024,768]{1,0:T(8,128)(2,1)} %get-tuple-element.51.o_ref, bf16[1024,768]{1,0:T(8,128)(2,1)} %bitcast.72, ...), custom_call_target="tpu_custom_call" | custom-call | flops 6643777536 | bytes 10485760 | tf_op jit(solution)/shard_map/pallas_call | solution.py:731
  128.3 18.3 %shard_map.156 = (bf16[1024,2304]{1,0:T(8,128)(2,1)}, bf16[1024,768]{1,0:T(8,128)(2,1)}, f32[1024,768]{1,0:T(8,128)}, bf16[1024,768]{1,0:T(8,128)(2,1)}, f32[1,768]{1,0:T(1,128)}) custom-call(bf16[1024,768]{1,0:T(8,128)(2,1)} %bitcast.79, f32[1024,768]{1,0:T(8,128)} %get-tuple-element.56.x1_ref, bf16[1024,1152]{1,0:T(8,128)(2,1)} %get-tuple-element.57.slope_ref, ...), custom_call_target="tpu_custom_call" | custom-call | flops 6643777536 | bytes 10485760 | tf_op jit(solution)/shard_map/pallas_call | solution.py:739
  146.6 7.8 %convolution_convert_fusion = bf16[768,2304]{1,0:T(8,128)(2,1)} fusion(bf16[1024,768]{1,0:T(8,128)(2,1)S(1)} %copy-done.16, bf16[1024,2304]{1,0:T(8,128)(2,1)} %get-tuple-element.65), kind=kOutput, calls=%fused_computation | convolution fusion | flops 3625648128 | bytes 9830400 | tf_op jit(solution)/shard_map/dot_general | solution.py:35
  154.5 2.5 convolution_convert_fusion.5
  156.9 3.3 convolution_convert_fusion.1
  160.2 51.7 %shard_map.157 = (bf16[1024,768]{1,0:T(8,128)(2,1)}, bf16[1024,768]{1,0:T(8,128)(2,1)}, bf16[1024,768]{1,0:T(8,128)(2,1)}, bf16[4,256,768]{2,1,0:T(8,128)(2,1)},...) custom-call(bf16[1024,2304]{1,0:T(8,128)(2,1)} %get-tuple-element.50.q_ref.k_ref.v_ref, ...), custom_call_target="tpu_custom_call" | custom-call | flops 25769803776 | bytes 10485760 | tf_op jit(solution)/shard_map/pallas_call | solution.py:755
  211.9 4.0 %convolution_convert_fusion.2 = bf16[768,768]{1,0:T(8,128)(2,1)} fusion(bf16[1024,768]{1,0:T(8,128)(2,1)S(1)} %copy-done.13, bf16[1024,768]{1,0:T(8,128)(2,1)} %get-tuple-element.69.dv_ref), kind=kOutput, calls=%fused_computation.3 | convolution fusion | flops 1208549376 | bytes 4325376 | tf_op jit(solution)/shard_map/dot_general | solution.py:35
  215.9 2.5 convolution_convert_fusion.3
  218.4 2.5 convolution_convert_fusion.4
  220.9 10.2 %shard_map.158 = (bf16[1024,768]{1,0:T(8,128)(2,1)}, f32[1,768]{1,0:T(1,128)}) custom-call(bf16[1024,768]{1,0:T(8,128)(2,1)} %get-tuple-element.67.dq_ref, bf16[1024,768]{1,0:T(8,128)(2,1)} %get-tuple-element.68.dk_ref, bf16[1024,768]{1,0:T(8,128)(2,1)} %get-tuple-element.69.dv_ref, bf16[1024,768]{1,0:T(8,128)(2,1)} %bitcast.73, ...), custom_call_target="tpu_custom_call" | custom-call | flops 3623878656 | bytes 10485760 | tf_op jit(solution)/shard_map/pallas_call | solution.py:769
  231.1 1.4 maximum_maximum_fusion.gains_ref
  232.5 90.7 %shard_map.159 = (bf16[4,256,768]{2,1,0:T(8,128)(2,1)}, bf16[288,768]{1,0:T(8,128)(2,1)}, bf16[192,768]{1,0:T(8,128)(2,1)}, bf16[192,2304]{1,0:T(8,128)(2,1)}, b...) custom-call(bf16[4,256,768]{2,1,0:T(8,128)(2,1)} %bitcast.46, ...), custom_call_target="tpu_custom_call" | custom-call | tf_op jit(solution)/shard_map/pallas_call | solution.py:782
  323.2 2.6 maximum_convert_fusion
  325.8 1.9 convert.2
  327.8 1.3 convert_element_type.62
  330.9 1.4 fusion.2
  332.3 1.1 copy.23
  (58 shorter events, 7.3 us)
Async XLA Ops:
  5.1 2.6 copy-start.8
  5.1 2.6 copy-start.9
  8.5 0.6 copy-start.5
  74.6 1.0 copy-start.6
  128.3 18.3 %copy-start.16 = (bf16[1024,768]{1,0:T(8,128)(2,1)S(1)}, bf16[1024,768]{1,0:T(8,128)(2,1)}, u32[]{:S(2)}) copy-start(bf16[1024,768]{1,0:T(8,128)(2,1)} %get-tuple-element.64) | copy-start | bytes 4718596
  146.6 7.8 %copy-start.14 = (bf16[1024,768]{1,0:T(8,128)(2,1)S(1)}, bf16[1024,768]{1,0:T(8,128)(2,1)}, u32[]{:S(2)}) copy-start(bf16[1024,768]{1,0:T(8,128)(2,1)} %get-tuple-element.51.o_ref) | copy-start | bytes 4718596
  146.6 7.8 %copy-start.15 = (bf16[1024,768]{1,0:T(8,128)(2,1)S(1)}, bf16[1024,768]{1,0:T(8,128)(2,1)}, u32[]{:S(2)}) copy-start(bf16[1024,768]{1,0:T(8,128)(2,1)} %get-tuple-element.63) | copy-start | bytes 4718596
  154.4 2.5 copy-start.10
  154.4 2.5 copy-start.17
  160.2 51.7 %copy-start.13 = (bf16[1024,768]{1,0:T(8,128)(2,1)S(1)}, bf16[1024,768]{1,0:T(8,128)(2,1)}, u32[]{:S(2)}) copy-start(bf16[1024,768]{1,0:T(8,128)(2,1)} %get-tuple-element.77) | copy-start | bytes 4718596
  211.9 4.0 %copy-start.12 = (bf16[1024,768]{1,0:T(8,128)(2,1)S(1)}, bf16[1024,768]{1,0:T(8,128)(2,1)}, u32[]{:S(2)}) copy-start(bf16[1024,768]{1,0:T(8,128)(2,1)} %get-tuple-element.68.dk_ref) | copy-start | bytes 4718596
  215.9 2.5 copy-start.11
  220.9 10.2 %copy-start.7 = (f32[1,768]{1,0:T(1,128)S(1)}, f32[1,768]{1,0:T(1,128)}, u32[]{:S(2)}) copy-start(f32[1,768]{1,0:T(1,128)} %get-tuple-element.73) | copy-start | bytes 9220
  323.2 2.6 copy-start.1
  325.8 1.9 copy-start.2
  327.8 1.3 copy-start.3
  327.8 2.3 copy-start.4
  329.1 3.3 copy-start
